TPU v7x, 512 devices: a whole 4x4x16 slice. The times are simulated.
512 devices in a mesh: blk: 8 (over z_hi, y), expert: 32 (over z_lo, x), tp: 2 (over core).
Axes of the slice: x: 4, y: 4, z: 16 (z_hi: 2, z_lo: 8; z = z_hi * 8 + z_lo), core: 2. Of those that a mesh axis runs over, the one named last changes fastest.
Arguments:
- tokens: bfloat16 [4096, 1536], P(('blk', 'expert')), may hold values from -6 to 6
- w_query: bfloat16 [1536, 1536], P('expert', 'tp'), may hold values from -0.15625 to 0.15625
- w_key: bfloat16 [1536, 512], P('expert', 'tp'), may hold values from -2.5 to 2.5
- w_value: bfloat16 [1536, 512], P('expert', 'tp'), may hold values from -0.15625 to 0.15625
- w_out: bfloat16 [1536, 1536], P('tp', 'expert'), may hold values from -0.15625 to 0.15625
- cache_keys: bfloat16 [64, 1024, 512], P('expert', 'blk', 'tp'), may hold values from -3840 to 3840, as said below
- cache_values: bfloat16 [64, 1024, 512], P('expert', 'blk', 'tp'), may hold values from -6 to 6
- parents: int32 [64, 64], P('expert'), may hold values from -1 to 62, as said below
- lengths: int32 [64], P('expert'), may hold values from 1 to 960, as said below
- accepted_leaf: int32 [64], P('expert'), may hold values from 0 to 63
- routes: int32 [4096, 8], P(('blk', 'expert')), may hold values from 0 to 31, all different within a row; in each aligned block of 16 rows (0 to 15, 16 to 31, ...) at most 6 rows name the same one
- route_weight: float32 [4096, 8], P(('blk', 'expert')), may hold values from 0.05 to 0.3
- w_gateup: bfloat16 [32, 1536, 2, 512], P('expert', None, None, 'tp'), may hold values from -0.15625 to 0.15625
- w_down: bfloat16 [32, 512, 1536], P('expert', 'tp'), may hold values from -0.25 to 0.25
Outputs:
- attended: bfloat16 [4096, 1536], P(('blk', 'expert'))
- expert_mix: bfloat16 [4096, 1536], P(('blk', 'expert'))
- new_keys: bfloat16 [64, 1024, 512], P('expert', 'blk', 'tp')
- new_values: bfloat16 [64, 1024, 512], P('expert', 'blk', 'tp')
Inputs may be any that keep to these rules, and one draw needn't show every extreme that they name: `cache_keys`: entries are finite and within the range. `parents`: token 0 of each request is the root, with parent -1; every other token's parent is a token of the same request with a lower index. `lengths`: each request's cache leaves room for its whole tree; some request has exactly 960 cached positions. `routes`: within the rows of one device (aligned blocks of 16 rows) no expert is named by more than 6 rows, a bound that some block reaches; the experts of a row differ.
All inputs are finite; a program needn't handle non-finite values.
Results may differ from a plain program's by a relative error of at most 0.02.
Values may be sent and summed in bfloat16 or wider, within the bound.
A program may use at most 64 MiB of HBM per device.

v0:
```python
import jax
import jax.numpy as jnp
from jax import lax
from jax.sharding import PartitionSpec as P

HD = 64
EXPERTS = 32


score_scale = 0.015625
residual_scale = 0.22
masked_score = -1e30
rope_base = 10000.0


def passed_along(value, axis, steps):
    count = lax.axis_size(axis)
    pairs = [(source, (source + steps) % count) for source in range(count)]
    return lax.ppermute(value, axis, pairs)


def ancestry(parents):
    tree_size = parents.shape[-1]
    columns = jnp.arange(tree_size, dtype=jnp.int32)
    parent_map = (parents[..., :, None] == columns).astype(jnp.float32)
    reached = jnp.minimum(jnp.eye(tree_size, dtype=jnp.float32) + parent_map, 1.0)
    for squaring in range(tree_size.bit_length()):
        longer = jnp.einsum("rij,rjk->rik", reached, reached, precision=lax.Precision.HIGHEST)
        reached = jnp.minimum(reached + longer, 1.0)
    return reached


def rms_norm(values):
    widened = values.astype(jnp.float32)
    scale_row = lax.rsqrt(jnp.mean(widened * widened, axis=-1, keepdims=True) + 1e-06)
    return (widened * scale_row).astype(jnp.bfloat16)


def rotary(values, positions):
    half_size = values.shape[-1] // 2
    frequency = rope_base ** (-(jnp.arange(half_size, dtype=jnp.float32) / half_size))
    angles = positions.astype(jnp.float32)[:, None] * frequency[None, :]
    cosine_part = jnp.cos(angles)[:, None, :]
    sine_part = jnp.sin(angles)[:, None, :]
    first_half = values[..., :half_size]
    second_half = values[..., half_size:]
    return jnp.concatenate(
        [
            first_half * cosine_part - second_half * sine_part,
            second_half * cosine_part + first_half * sine_part,
        ],
        -1,
    )


def attend_block(query_block, key_block, value_block, usable):
    scores = (
        jnp.einsum("nqhgd,nkhd->nqhgk", query_block, key_block, preferred_element_type=jnp.float32)
        * score_scale
    )
    scores = jnp.where(usable, scores, masked_score)
    peak_score = jnp.max(scores, axis=-1)
    weights = jnp.where(usable, jnp.exp(scores - peak_score[..., None]), 0.0)
    weight_high = weights.astype(jnp.bfloat16)
    weight_low = (weights - weight_high.astype(jnp.float32)).astype(jnp.bfloat16)
    acc_part = jnp.einsum(
        "nqhgk,nkhd->nqhgd", weight_high, value_block, preferred_element_type=jnp.float32
    ) + jnp.einsum("nqhgk,nkhd->nqhgd", weight_low, value_block, preferred_element_type=jnp.float32)
    return (peak_score, jnp.sum(weights, -1), acc_part)


def combine_parts(former, latter):
    peak_score = jnp.maximum(former[0], latter[0])
    scale_one = jnp.exp(former[0] - peak_score)
    scale_two = jnp.exp(latter[0] - peak_score)
    return (
        peak_score,
        former[1] * scale_one + latter[1] * scale_two,
        former[2] * scale_one[..., None] + latter[2] * scale_two[..., None],
    )


def local(
    tokens,
    w_query,
    w_key,
    w_value,
    w_out,
    cache_keys,
    cache_values,
    parents,
    lengths,
    accepted_leaf,
    routes,
    route_weight,
    w_gateup,
    w_down,
):
    row_count = tokens.shape[0]
    model_width = tokens.shape[1]
    blk_count = lax.axis_size("blk")
    blk_rank = lax.axis_index("blk")
    req_count = parents.shape[0]
    tree_size = parents.shape[1]
    part_size = row_count // req_count
    head_size = HD
    head_count = w_query.shape[1] // head_size
    kv_count = w_key.shape[1] // head_size
    group_size = head_count // kv_count
    block_len = cache_keys.shape[1]
    kv_cols = kv_count * head_size
    reached = ancestry(parents)
    depths = (jnp.sum(reached, -1) - 1.0).astype(jnp.int32)
    slot_start = blk_rank * part_size
    own_depths = lax.dynamic_slice_in_dim(depths, slot_start, part_size, 1)
    positions = (lengths[:, None] + own_depths).reshape(-1)
    normed = rms_norm(tokens)
    query_raw = jnp.dot(
        normed,
        lax.all_gather(w_query, "expert", axis=0, tiled=True),
        preferred_element_type=jnp.float32,
    )
    key_raw = jnp.dot(
        normed,
        lax.all_gather(w_key, "expert", axis=0, tiled=True),
        preferred_element_type=jnp.float32,
    )
    value_raw = jnp.dot(
        normed,
        lax.all_gather(w_value, "expert", axis=0, tiled=True),
        preferred_element_type=jnp.float32,
    )
    own_queries = rotary(query_raw.reshape(row_count, head_count, head_size), positions).astype(
        jnp.bfloat16
    )
    key_rows = rotary(key_raw.reshape(row_count, kv_count, head_size), positions).astype(
        jnp.bfloat16
    )
    value_rows = value_raw.astype(jnp.bfloat16)
    tree_keys, tree_values = (
        lax.all_gather(key_rows.reshape(req_count, part_size, kv_cols), "blk", axis=1, tiled=True),
        lax.all_gather(
            value_rows.reshape(req_count, part_size, kv_cols), "blk", axis=1, tiled=True
        ),
    )
    own_query = own_queries.reshape(req_count, part_size, kv_count, group_size, head_size)
    own_reach = lax.dynamic_slice_in_dim(reached, slot_start, part_size, 1)
    running = attend_block(
        own_query,
        tree_keys.reshape(req_count, tree_size, kv_count, head_size),
        tree_values.reshape(req_count, tree_size, kv_count, head_size),
        (own_reach > 0.5)[:, :, None, None, :],
    )
    moving_keys = cache_keys
    moving_values = cache_values
    for turn_index in range(blk_count):
        source = (blk_rank - turn_index) % blk_count
        cache_pos = source * block_len + jnp.arange(block_len, dtype=jnp.int32)
        usable = (cache_pos[None, :] < lengths[:, None])[:, None, None, None, :]
        outcome = attend_block(
            own_query,
            moving_keys.reshape(req_count, block_len, kv_count, head_size),
            moving_values.reshape(req_count, block_len, kv_count, head_size),
            usable,
        )
        running = combine_parts(running, outcome)
        if turn_index + 1 < blk_count:
            moving_keys, moving_values = passed_along((moving_keys, moving_values), "blk", 1)
    context = (
        (running[2] / running[1][..., None])
        .reshape(row_count, head_count * head_size)
        .astype(jnp.bfloat16)
    )
    head_terms = jnp.dot(
        context,
        lax.all_gather(w_out, "expert", axis=1, tiled=True),
        preferred_element_type=jnp.float32,
    )
    attended = lax.psum(head_terms.astype(jnp.bfloat16), "tp")
    hidden_in = rms_norm(tokens.astype(jnp.float32) + residual_scale * attended.astype(jnp.float32))
    top_count = routes.shape[1]
    expert_total = EXPERTS
    local_experts = w_gateup.shape[0]
    capacity = max(2, 3 * row_count * top_count // (2 * expert_total))
    flat_route = routes.reshape(-1)
    choose_map = (flat_route[:, None] == jnp.arange(expert_total, dtype=jnp.int32)[None, :]).astype(
        jnp.int32
    )
    earlier_count = jnp.sum((jnp.cumsum(choose_map, 0) - choose_map) * choose_map, 1)
    slot_index = flat_route * capacity + earlier_count
    source_row = jnp.arange(flat_route.shape[0], dtype=jnp.int32) // top_count
    outgoing = (
        jnp.zeros((expert_total * capacity, model_width), jnp.bfloat16)
        .at[slot_index]
        .set(hidden_in[source_row])
    )
    outgoing = outgoing.reshape(expert_total // local_experts, local_experts, capacity, model_width)
    gate_up = jnp.einsum(
        "sxcd,xdgf->sxcgf",
        lax.all_to_all(outgoing, "expert", split_axis=0, concat_axis=0, tiled=True),
        w_gateup,
        preferred_element_type=jnp.float32,
    )
    expert_hidden = (jax.nn.silu(gate_up[:, :, :, 0, :]) * gate_up[:, :, :, 1, :]).astype(
        jnp.bfloat16
    )
    partial_out = jnp.einsum(
        "sxcf,xfd->sxcd", expert_hidden, w_down, preferred_element_type=jnp.float32
    )
    summed = lax.psum(partial_out.astype(jnp.bfloat16), "tp")
    sent_home = lax.all_to_all(summed, "expert", split_axis=0, concat_axis=0, tiled=True)
    column_width = sent_home.shape[-1]
    picked = sent_home.reshape(expert_total * capacity, column_width)[slot_index].reshape(
        row_count, top_count, column_width
    )
    expert_mix = jnp.sum(route_weight[:, :, None] * picked.astype(jnp.float32), 1).astype(
        jnp.bfloat16
    )
    leaf_pick = (jnp.arange(tree_size, dtype=jnp.int32)[None, :] == accepted_leaf[:, None]).astype(
        jnp.float32
    )
    path_mask = jnp.sum(leaf_pick[:, :, None] * reached, 1)
    target_pos = lengths[:, None] + depths
    block_pos = blk_rank * block_len + jnp.arange(block_len, dtype=jnp.int32)
    placing_mask = (block_pos[None, :, None] == target_pos[:, None, :]) & (
        path_mask[:, None, :] > 0.5
    )
    written = jnp.any(placing_mask, -1)
    placing = placing_mask.astype(jnp.bfloat16)
    moved_keys = jnp.einsum(
        "rpt,rtc->rpc", placing, tree_keys, preferred_element_type=jnp.float32
    ).astype(jnp.bfloat16)
    moved_values = jnp.einsum(
        "rpt,rtc->rpc", placing, tree_values, preferred_element_type=jnp.float32
    ).astype(jnp.bfloat16)
    new_keys = jnp.where(written[:, :, None], moved_keys, cache_keys)
    new_values = jnp.where(written[:, :, None], moved_values, cache_values)
    return (attended, expert_mix, new_keys, new_values)


def solution(mesh):
    in_specs = (
        P(("blk", "expert"), None),
        P("expert", "tp"),
        P("expert", "tp"),
        P("expert", "tp"),
        P("tp", "expert"),
        P("expert", "blk", "tp"),
        P("expert", "blk", "tp"),
        P("expert", None),
        P("expert"),
        P("expert"),
        P(("blk", "expert"), None),
        P(("blk", "expert"), None),
        P("expert", None, None, "tp"),
        P("expert", "tp", None),
    )
    out_specs = (
        P(("blk", "expert"), None),
        P(("blk", "expert"), None),
        P("expert", "blk", "tp"),
        P("expert", "blk", "tp"),
    )
    return jax.shard_map(local, mesh=mesh, in_specs=in_specs, out_specs=out_specs, check_vma=False)
```

profile of v0, /device:TPU:1, one launch (start us, length us, event | category | flops | bytes accessed | tf_op | source)
XLA Modules:
  0.0 709.5 jit_solution(18223612820131724418)
XLA Ops:
  8.0 4.0 collective-permute-start
  12.1 3.2 collective-permute-start.1
  20.3 117.4 %all_gather.20 = bf16[1536,256]{1,0:T(8,128)(2,1)S(1)} all-gather(bf16[48,256]{1,0:T(8,128)(2,1)} %param.16), channel_id=1, replica_groups=mesh['blk'=8,'expert'=32,'tp'=2] {'expert'}, dimensions={0}, use_global_device_ids=true | all-gather | bytes 811008 | tf_op jit(solution)/shard_map/all_gather | solution.py:125
  138.1 104.7 %all_gather.18 = bf16[1536,256]{1,0:T(8,128)(2,1)S(1)} all-gather(bf16[48,256]{1,0:T(8,128)(2,1)S(1)} %copy-done.9), channel_id=1, replica_groups=mesh['blk'=8,'expert'=32,'tp'=2] {'expert'}, dimensions={0}, use_global_device_ids=true | all-gather | bytes 811008 | tf_op jit(solution)/shard_map/all_gather | solution.py:130
  243.5 1.9 collective-permute-start.2
  245.4 7.7 %collective-permute-start.3 = (bf16[2,128,256]{2,1,0:T(8,128)(2,1)S(1)}, bf16[2,128,256]{2,1,0:T(8,128)(2,1)S(1)}, u32[]{:S(2)}, u32[]{:S(2)}) collective-permute-start(bf16[2,128,256]{2,1,0:T(8,128)(2,1)S(1)} %collective-permute-done.1), channel_id=1, source_target_pairs={{0,64},{64,128},{128,192},{192,256},{256,320},{320,384},{384,448},... | collective-permute-start | bytes 393224 | tf_op jit(solution)/shard_map/ppermute | solution.py:19
  253.7 27.7 %collective-permute-done.2 = bf16[2,128,256]{2,1,0:T(8,128)(2,1)S(1)} collective-permute-done((bf16[2,128,256]{2,1,0:T(8,128)(2,1)S(1)}, bf16[2,128,256]{2,1,0:T(8,128)(2,1)S(1)}, u32[]{:S(2)}, u32[]{:S(2)}) %collective-permute-start.2) | collective-permute-done | bytes 131104 | tf_op jit(solution)/shard_map/ppermute | solution.py:19
  281.3 1.9 collective-permute-start.4
  283.2 1.9 collective-permute-start.5
  285.2 21.9 %collective-permute-done.4 = bf16[2,128,256]{2,1,0:T(8,128)(2,1)S(1)} collective-permute-done((bf16[2,128,256]{2,1,0:T(8,128)(2,1)S(1)}, bf16[2,128,256]{2,1,0:T(8,128)(2,1)S(1)}, u32[]{:S(2)}, u32[]{:S(2)}) %collective-permute-start.4) | collective-permute-done | bytes 131104 | tf_op jit(solution)/shard_map/ppermute | solution.py:19
  307.1 1.9 collective-permute-start.6
  309.0 1.9 collective-permute-start.7
  311.2 16.5 %collective-permute-done.6 = bf16[2,128,256]{2,1,0:T(8,128)(2,1)S(1)} collective-permute-done((bf16[2,128,256]{2,1,0:T(8,128)(2,1)S(1)}, bf16[2,128,256]{2,1,0:T(8,128)(2,1)S(1)}, u32[]{:S(2)}, u32[]{:S(2)}) %collective-permute-start.6) | collective-permute-done | bytes 131104 | tf_op jit(solution)/shard_map/ppermute | solution.py:19
  327.7 1.9 collective-permute-start.8
  330.7 1.9 collective-permute-start.9
  333.0 13.8 %collective-permute-done.8 = bf16[2,128,256]{2,1,0:T(8,128)(2,1)S(1)} collective-permute-done((bf16[2,128,256]{2,1,0:T(8,128)(2,1)S(1)}, bf16[2,128,256]{2,1,0:T(8,128)(2,1)S(1)}, u32[]{:S(2)}, u32[]{:S(2)}) %collective-permute-start.8) | collective-permute-done | bytes 131104 | tf_op jit(solution)/shard_map/ppermute | solution.py:19
  346.8 1.9 collective-permute-start.10
  348.8 1.9 collective-permute-start.11
  350.7 70.6 %all_gather.21 = bf16[2,64,256]{2,1,0:T(8,128)(2,1)S(1)} all-gather(bf16[2,8,256]{2,1,0:T(8,128)(2,1)S(1)} %convert_element_type.196), channel_id=1, replica_groups=mesh['blk'=8,'expert'=32,'tp'=2] {'blk'}, dimensions={1}, use_global_device_ids=true | all-gather | bytes 73728 | tf_op jit(solution)/shard_map/all_gather | solution.py:141
  421.4 1.9 collective-permute-start.12
  423.4 1.9 collective-permute-start.13
  425.3 60.9 %all_gather.19 = bf16[2,64,256]{2,1,0:T(8,128)(2,1)S(1)} all-gather(bf16[2,8,256]{2,1,0:T(8,128)(2,1)S(1)} %fusion.69), channel_id=1, replica_groups=mesh['blk'=8,'expert'=32,'tp'=2] {'blk'}, dimensions={1}, use_global_device_ids=true | all-gather | bytes 73728 | tf_op jit(solution)/shard_map/all_gather | solution.py:142
  494.6 2.1 fusion.223
  505.4 2.4 convolution_convert_fusion.1
  507.8 50.6 %psum.14 = bf16[16,1536]{1,0:T(8,128)(2,1)S(1)} all-reduce(bf16[16,1536]{1,0:T(8,128)(2,1)S(1)} %convolution_convert_fusion.1), channel_id=1, replica_groups=mesh['blk'=8,'expert'=32,'tp'=2] {'tp'}, use_global_device_ids=true, to_apply=%region_20.21 | all-reduce | flops 24576 | bytes 98304 | tf_op jit(solution)/shard_map/psum | solution.py:179
  558.7 2.7 scatter_custom_fusion
  561.5 42.6 %all_to_all.10 = bf16[32,1,6,1536]{3,2,1,0:T(8,128)(2,1)S(1)} all-to-all(bf16[32,1,6,1536]{3,2,1,0:T(8,128)(2,1)S(1)} %bitcast.263), channel_id=1, replica_groups=mesh['blk'=8,'expert'=32,'tp'=2] {'expert'}, dimensions={0} | all-to-all | bytes 1179648 | tf_op jit(solution)/shard_map/all_to_all | solution.py:200
  604.1 1.9 fusion.4
  607.2 40.7 %all-reduce.2.cloned.1.call-done = bf16[32,1,6,1536]{3,0,2,1:T(8,128)(2,1)} async-done(((bf16[32,1,6,1536]{3,0,2,1:T(8,128)(2,1)}), bf16[32,1,6,1536]{3,0,2,1:T(8,128)(2,1)}) %all-reduce.2.cloned.1.call-update) | async-done | bytes 589840 | tf_op jit(solution)/shard_map/psum | solution.py:210
  647.9 2.3 copy.99
  650.1 11.5 %all-to-all-start.1 = ((bf16[32,1,6,1536]{3,2,1,0:T(8,128)(2,1)}), bf16[32,1,6,1536]{3,2,1,0:T(8,128)(2,1)S(1)}, u32[]{:S(2)}, u32[]{:S(2)}) async-start(bf16[32,1,6,1536]{3,2,1,0:T(8,128)(2,1)} %copy.99), calls=%async_computation.1 | async-start | bytes 1572864 | tf_op jit(solution)/shard_map/all_to_all | solution.py:211
  663.9 37.0 %all-to-all-done.1 = bf16[32,1,6,1536]{3,2,1,0:T(8,128)(2,1)S(1)} async-done(((bf16[32,1,6,1536]{3,2,1,0:T(8,128)(2,1)}), bf16[32,1,6,1536]{3,2,1,0:T(8,128)(2,1)S(1)}, u32[]{:S(2)}, u32[]{:S(2)}) %all-to-all-start.1) | async-done | bytes 589856 | tf_op jit(solution)/shard_map/all_to_all | solution.py:211
  (162 shorter events, 31.7 us)
Async XLA Ops:
  7.2 598.9 %copy-start = (bf16[1,256,1536]{2,1,0:T(8,128)(2,1)S(1)}, bf16[1,256,1536]{2,1,0:T(8,128)(2,1)}, u32[]{:S(2)}) copy-start(bf16[1,256,1536]{2,1,0:T(8,128)(2,1)} %param.27) | copy-start | bytes 2359300
  7.2 236.2 %copy-start.11 = (s32[2]{0:T(128)S(1)}, s32[2]{0:T(128)}, u32[]{:S(2)}) copy-start(s32[2]{0:T(128)} %param.22) | copy-start | bytes 28
  7.2 130.5 %copy-start.1 = (bf16[16,1536]{1,0:T(8,128)(2,1)S(1)}, bf16[16,1536]{1,0:T(8,128)(2,1)}, u32[]{:S(2)}) copy-start(bf16[16,1536]{1,0:T(8,128)(2,1)} %param.14) | copy-start | bytes 147460
  7.2 130.9 %copy-start.9 = (bf16[48,256]{1,0:T(8,128)(2,1)S(1)}, bf16[48,256]{1,0:T(8,128)(2,1)}, u32[]{:S(2)}) copy-start(bf16[48,256]{1,0:T(8,128)(2,1)} %param.17) | copy-start | bytes 73732
  7.2 235.7 %copy-start.10 = (s32[16,8]{0,1:T(8,128)S(1)}, s32[16,8]{0,1:T(8,128)}, u32[]{:S(2)}) copy-start(s32[16,8]{0,1:T(8,128)} %param.24) | copy-start | bytes 1540
  7.2 487.4 %all-gather.3.cloned.1.call-start = ((), (), s32[]{:S(2)}) async-start(), calls=%async_computation.2 | async-start | bytes 2433024 | tf_op jit(solution)/shard_map/all_gather | solution.py:120
  8.0 497.5 %all-gather.5.cloned.1.call-start = ((), (), s32[]{:S(2)}) async-start(), calls=%async_computation.3 | async-start | bytes 2433024 | tf_op jit(solution)/shard_map/all_gather | solution.py:176
  8.0 235.5 %collective-permute-start = (bf16[2,128,256]{2,1,0:T(8,128)(2,1)}, bf16[2,128,256]{2,1,0:T(8,128)(2,1)S(1)}, u32[]{:S(2)}, u32[]{:S(2)}) collective-permute-start(bf16[2,128,256]{2,1,0:T(8,128)(2,1)} %param.19), channel_id=1, source_target_pairs={{0,64},{64,128},{128,192},{192,256},{256,320},{320,384},{384,448},... | collective-permute-start | bytes 393224 | tf_op jit(solution)/shard_map/ppermute | solution.py:19
  12.1 233.3 %collective-permute-start.1 = (bf16[2,128,256]{2,1,0:T(8,128)(2,1)}, bf16[2,128,256]{2,1,0:T(8,128)(2,1)S(1)}, u32[]{:S(2)}, u32[]{:S(2)}) collective-permute-start(bf16[2,128,256]{2,1,0:T(8,128)(2,1)} %param.20), channel_id=1, source_target_pairs={{0,64},{64,128},{128,192},{192,256},{256,320},{320,384},{384,448},... | collective-permute-start | bytes 393224 | tf_op jit(solution)/shard_map/ppermute | solution.py:19
  15.3 632.6 %all-reduce.2.cloned.1.call-start = ((), (), s32[]{:S(2)}) async-start(), calls=%async_computation.4 | async-start | bytes 1179648 | tf_op jit(solution)/shard_map/psum | solution.py:210
  16.9 315.7 %copy-start.3 = (bf16[2,128,256]{2,1,0:T(8,128)(2,1)S(1)}, bf16[2,128,256]{2,1,0:T(8,128)(2,1)}, u32[]{:S(2)}) copy-start(bf16[2,128,256]{2,1,0:T(8,128)(2,1)} %param.19) | copy-start | bytes 393220
  17.4 315.5 %copy-start.4 = (bf16[2,128,256]{2,1,0:T(8,128)(2,1)S(1)}, bf16[2,128,256]{2,1,0:T(8,128)(2,1)}, u32[]{:S(2)}) copy-start(bf16[2,128,256]{2,1,0:T(8,128)(2,1)} %param.20) | copy-start | bytes 393220
  243.5 37.9 %collective-permute-start.2 = (bf16[2,128,256]{2,1,0:T(8,128)(2,1)S(1)}, bf16[2,128,256]{2,1,0:T(8,128)(2,1)S(1)}, u32[]{:S(2)}, u32[]{:S(2)}) collective-permute-start(bf16[2,128,256]{2,1,0:T(8,128)(2,1)S(1)} %collective-permute-done), channel_id=1, source_target_pairs={{0,64},{64,128},{128,192},{192,256},{256,320},{320,384},{384,448},... | collective-permute-start | bytes 393224 | tf_op jit(solution)/shard_map/ppermute | solution.py:19
  245.4 37.8 %collective-permute-start.3 = (bf16[2,128,256]{2,1,0:T(8,128)(2,1)S(1)}, bf16[2,128,256]{2,1,0:T(8,128)(2,1)S(1)}, u32[]{:S(2)}, u32[]{:S(2)}) collective-permute-start(bf16[2,128,256]{2,1,0:T(8,128)(2,1)S(1)} %collective-permute-done.1), channel_id=1, source_target_pairs={{0,64},{64,128},{128,192},{192,256},{256,320},{320,384},{384,448},... | collective-permute-start | bytes 393224 | tf_op jit(solution)/shard_map/ppermute | solution.py:19
  281.3 25.8 %collective-permute-start.4 = (bf16[2,128,256]{2,1,0:T(8,128)(2,1)S(1)}, bf16[2,128,256]{2,1,0:T(8,128)(2,1)S(1)}, u32[]{:S(2)}, u32[]{:S(2)}) collective-permute-start(bf16[2,128,256]{2,1,0:T(8,128)(2,1)S(1)} %collective-permute-done.2), channel_id=1, source_target_pairs={{0,64},{64,128},{128,192},{192,256},{256,320},{320,384},{384,448},... | collective-permute-start | bytes 393224 | tf_op jit(solution)/shard_map/ppermute | solution.py:19
  283.2 25.8 %collective-permute-start.5 = (bf16[2,128,256]{2,1,0:T(8,128)(2,1)S(1)}, bf16[2,128,256]{2,1,0:T(8,128)(2,1)S(1)}, u32[]{:S(2)}, u32[]{:S(2)}) collective-permute-start(bf16[2,128,256]{2,1,0:T(8,128)(2,1)S(1)} %collective-permute-done.3), channel_id=1, source_target_pairs={{0,64},{64,128},{128,192},{192,256},{256,320},{320,384},{384,448},... | collective-permute-start | bytes 393224 | tf_op jit(solution)/shard_map/ppermute | solution.py:19
  307.1 20.6 %collective-permute-start.6 = (bf16[2,128,256]{2,1,0:T(8,128)(2,1)S(1)}, bf16[2,128,256]{2,1,0:T(8,128)(2,1)S(1)}, u32[]{:S(2)}, u32[]{:S(2)}) collective-permute-start(bf16[2,128,256]{2,1,0:T(8,128)(2,1)S(1)} %collective-permute-done.4), channel_id=1, source_target_pairs={{0,64},{64,128},{128,192},{192,256},{256,320},{320,384},{384,448},... | collective-permute-start | bytes 393224 | tf_op jit(solution)/shard_map/ppermute | solution.py:19
  309.0 21.6 %collective-permute-start.7 = (bf16[2,128,256]{2,1,0:T(8,128)(2,1)S(1)}, bf16[2,128,256]{2,1,0:T(8,128)(2,1)S(1)}, u32[]{:S(2)}, u32[]{:S(2)}) collective-permute-start(bf16[2,128,256]{2,1,0:T(8,128)(2,1)S(1)} %collective-permute-done.5), channel_id=1, source_target_pairs={{0,64},{64,128},{128,192},{192,256},{256,320},{320,384},{384,448},... | collective-permute-start | bytes 393224 | tf_op jit(solution)/shard_map/ppermute | solution.py:19
  327.7 19.1 %collective-permute-start.8 = (bf16[2,128,256]{2,1,0:T(8,128)(2,1)S(1)}, bf16[2,128,256]{2,1,0:T(8,128)(2,1)S(1)}, u32[]{:S(2)}, u32[]{:S(2)}) collective-permute-start(bf16[2,128,256]{2,1,0:T(8,128)(2,1)S(1)} %collective-permute-done.6), channel_id=1, source_target_pairs={{0,64},{64,128},{128,192},{192,256},{256,320},{320,384},{384,448},... | collective-permute-start | bytes 393224 | tf_op jit(solution)/shard_map/ppermute | solution.py:19
  330.7 18.1 %collective-permute-start.9 = (bf16[2,128,256]{2,1,0:T(8,128)(2,1)S(1)}, bf16[2,128,256]{2,1,0:T(8,128)(2,1)S(1)}, u32[]{:S(2)}, u32[]{:S(2)}) collective-permute-start(bf16[2,128,256]{2,1,0:T(8,128)(2,1)S(1)} %collective-permute-done.7), channel_id=1, source_target_pairs={{0,64},{64,128},{128,192},{192,256},{256,320},{320,384},{384,448},... | collective-permute-start | bytes 393224 | tf_op jit(solution)/shard_map/ppermute | solution.py:19
  346.8 74.6 %collective-permute-start.10 = (bf16[2,128,256]{2,1,0:T(8,128)(2,1)S(1)}, bf16[2,128,256]{2,1,0:T(8,128)(2,1)}, u32[]{:S(2)}, u32[]{:S(2)}) collective-permute-start(bf16[2,128,256]{2,1,0:T(8,128)(2,1)S(1)} %collective-permute-done.8), channel_id=1, source_target_pairs={{0,64},{64,128},{128,192},{192,256},{256,320},{320,384},{384,448},... | collective-permute-start | bytes 393224 | tf_op jit(solution)/shard_map/ppermute | solution.py:19
  348.8 137.6 %copy-start.8 = (bf16[2,128,256]{2,1,0:T(8,128)(2,1)}, bf16[2,128,256]{2,1,0:T(8,128)(2,1)S(1)}, u32[]{:S(2)}) copy-start(bf16[2,128,256]{2,1,0:T(8,128)(2,1)S(1)} %collective-permute-done.9) | copy-start | bytes 393220
  348.8 74.6 %collective-permute-start.11 = (bf16[2,128,256]{2,1,0:T(8,128)(2,1)S(1)}, bf16[2,128,256]{2,1,0:T(8,128)(2,1)}, u32[]{:S(2)}, u32[]{:S(2)}) collective-permute-start(bf16[2,128,256]{2,1,0:T(8,128)(2,1)S(1)} %collective-permute-done.9), channel_id=1, source_target_pairs={{0,64},{64,128},{128,192},{192,256},{256,320},{320,384},{384,448},... | collective-permute-start | bytes 393224 | tf_op jit(solution)/shard_map/ppermute | solution.py:19
  421.4 71.1 %collective-permute-start.12 = (bf16[2,128,256]{2,1,0:T(8,128)(2,1)}, bf16[2,128,256]{2,1,0:T(8,128)(2,1)}, u32[]{:S(2)}, u32[]{:S(2)}) collective-permute-start(bf16[2,128,256]{2,1,0:T(8,128)(2,1)} %collective-permute-done.10), channel_id=1, source_target_pairs={{0,64},{64,128},{128,192},{192,256},{256,320},{320,384},{384,448},... | collective-permute-start | bytes 393224 | tf_op jit(solution)/shard_map/ppermute | solution.py:19
  423.4 70.2 %collective-permute-start.13 = (bf16[2,128,256]{2,1,0:T(8,128)(2,1)}, bf16[2,128,256]{2,1,0:T(8,128)(2,1)}, u32[]{:S(2)}, u32[]{:S(2)}) collective-permute-start(bf16[2,128,256]{2,1,0:T(8,128)(2,1)} %collective-permute-done.11), channel_id=1, source_target_pairs={{0,64},{64,128},{128,192},{192,256},{256,320},{320,384},{384,448},... | collective-permute-start | bytes 393224 | tf_op jit(solution)/shard_map/ppermute | solution.py:19
  497.0 3.9 copy-start.7
  497.3 3.8 copy-start.6
  497.8 3.5 copy-start.5
  558.4 47.6 %copy-start.2 = (bf16[16,1536]{1,0:T(8,128)(2,1)}, bf16[16,1536]{1,0:T(8,128)(2,1)S(1)}, u32[]{:S(2)}) copy-start(bf16[16,1536]{1,0:T(8,128)(2,1)S(1)} %psum.14) | copy-start | bytes 147460
  606.0 55.6 %copy-start.12 = (f32[16,8]{0,1:T(8,128)S(1)}, f32[16,8]{0,1:T(8,128)}, u32[]{:S(2)}) copy-start(f32[16,8]{0,1:T(8,128)} %param.25) | copy-start | bytes 1540
  650.1 50.7 %all-to-all-start.1 = ((bf16[32,1,6,1536]{3,2,1,0:T(8,128)(2,1)}), bf16[32,1,6,1536]{3,2,1,0:T(8,128)(2,1)S(1)}, u32[]{:S(2)}, u32[]{:S(2)}) async-start(bf16[32,1,6,1536]{3,2,1,0:T(8,128)(2,1)} %copy.99), calls=%async_computation.1 | async-start | bytes 1572864 | tf_op jit(solution)/shard_map/all_to_all | solution.py:211
Sparse Core Ops, SparseCore 0:
  10.1 210.4 all-gather.2
  222.7 239.4 all-gather.4
  607.3 40.4 all-reduce.1
where the time goes:
time: 712 us; the launch traced here: 709 us
  blocking collectives  447 us (63%)
  waiting for transfers between devices  159 us (22%)
  starting transfers between devices  47.7 us (7%)
  matrix products  19 us (3%)
  local copies, waits for them, and re-layouts  15.8 us (2%)
  between operations  14.7 us (2%)
    all_gather x1, blocking collectives, local(): lax.all_gather(w_key, 'expert', axis=0, tiled=True)  117 us
    all_gather x1, blocking collectives, local(): lax.all_gather(w_value, 'expert', axis=0, tiled=True)  105 us
    ppermute x14, waiting for transfers between devices, passed_along(): return lax.ppermute(value, axis, pairs)  80.9 us
    all_gather x1, blocking collectives, local(): lax.all_gather(key_rows.reshape(req_count, part_size, kv_cols), 'blk', ax...  70.6 us
    all_gather x1, blocking collectives, local(): lax.all_gather(value_rows.reshape(req_count, part_size, kv_cols), 'blk',...  60.9 us
    psum x1, blocking collectives, local(): attended = lax.psum(head_terms.astype(jnp.bfloat16), 'tp')  50.6 us
    all_to_all x1, blocking collectives, local(): lax.all_to_all(outgoing, 'expert', split_axis=0, concat_axis=0, tiled=True)  42.6 us
    psum x1, waiting for transfers between devices, local(): summed = lax.psum(partial_out.astype(jnp.bfloat16), 'tp')  40.7 us
  transfers between devices with their start and end apart: 18, of which 7 were waited for; matrix products, arithmetic and copies ran while one was open for 4% of the time, Pallas kernels for 0%

commit v1 on v0

--- a/solution.py
+++ b/solution.py
@@ -1,10 +1,11 @@
 import jax
 import jax.numpy as jnp
 from jax import lax
+from jax.experimental import pallas as pl
+from jax.experimental.pallas import tpu as pltpu
 from jax.sharding import PartitionSpec as P
 
 HD = 64
-EXPERTS = 32
 
 
 score_scale = 0.015625
@@ -78,6 +79,176 @@
         former[1] * scale_one + latter[1] * scale_two,
         former[2] * scale_one[..., None] + latter[2] * scale_two[..., None],
     )
+
+
+D_MODEL = 1536
+HALF = 768
+SLOTS = 32
+OWN_SLOT = 12
+SLAB = 8
+MESH = pl.DeviceIdType.MESH
+
+
+def moe_kernel(hid_ref, routes_ref, weight_ref, wgu_hbm, wdn_hbm, out_ref, wgu, wdn, send, recv, pair_send,
+               pair_recv, back_send, back_recv, fin_send, fin_recv, load_sem, out_sem, in_sem, swap_sem):
+    blk = lax.axis_index("blk")
+    exp = lax.axis_index("expert")
+    tp = lax.axis_index("tp")
+    z = (blk // 4) * 8 + exp // 4
+    y = blk % 4
+    x = exp % 4
+
+    def plane(dz, dx):
+        zz = (z + dz + 16) % 16
+        return ((zz // 8) * 4 + y, (zz % 8) * 4 + (x + dx) % 4, tp)
+
+    sibling = (blk, exp, 1 - tp)
+    loads = [
+        pltpu.make_async_copy(wgu_hbm, wgu, load_sem.at[0]),
+        pltpu.make_async_copy(wdn_hbm, wdn, load_sem.at[1]),
+    ]
+    for load in loads:
+        load.start()
+
+    barrier = pltpu.get_barrier_semaphore()
+
+    def greet(i, carry):
+        q = i + (i + 20) // 36
+        pl.semaphore_signal(barrier, inc=1, device_id=plane(q // 4 - 4, q % 4), device_id_type=MESH)
+        return carry
+
+    lax.fori_loop(0, 35, greet, 0)
+    pl.semaphore_signal(barrier, inc=1, device_id=sibling, device_id_type=MESH)
+
+    rows = hid_ref.shape[0]
+    mine = pl.ds(pl.multiple_of(tp * HALF, HALF), HALF)
+    theirs = pl.ds(pl.multiple_of((1 - tp) * HALF, HALF), HALF)
+    slot = lax.broadcasted_iota(jnp.int32, (SLOTS * SLAB, rows), 0)
+    kk = slot // SLAB
+    cc = slot % SLAB
+    expert_of = ((exp // 4 + kk // 4 + 5) % 8) * 4 + (x + kk % 4) % 4
+    named = jnp.zeros((SLOTS * SLAB, rows), jnp.float32)
+    weighed = jnp.zeros((SLOTS * SLAB, rows), jnp.float32)
+    for t in range(8):
+        hit = expert_of == routes_ref[t : t + 1, :]
+        named = named + jnp.where(hit, 1.0, 0.0)
+        weighed = weighed + jnp.where(hit, weight_ref[t : t + 1, :], 0.0)
+    earlier = jnp.where(
+        lax.broadcasted_iota(jnp.int32, (rows, rows), 0) < lax.broadcasted_iota(jnp.int32, (rows, rows), 1), 1.0, 0.0
+    ).astype(jnp.bfloat16)
+    rank = jnp.dot(named.astype(jnp.bfloat16), earlier, preferred_element_type=jnp.float32)
+    chosen = jnp.where((named > 0.5) & (jnp.abs(rank - cc.astype(jnp.float32)) < 0.5), 1.0, 0.0)
+    weighed = weighed * chosen
+    packed = jnp.dot(chosen.astype(jnp.bfloat16), hid_ref[:, mine], preferred_element_type=jnp.float32)
+    send[...] = packed.astype(jnp.bfloat16).reshape(SLOTS, SLAB, HALF)
+    recv[tp, OWN_SLOT] = packed[OWN_SLOT * SLAB : (OWN_SLOT + 1) * SLAB].astype(jnp.bfloat16)
+    pl.semaphore_wait(barrier, 36)
+
+    def ship(i, carry):
+        k = i + (i + 20) // 32
+        pltpu.make_async_remote_copy(
+            src_ref=send.at[k], dst_ref=recv.at[tp, k], send_sem=out_sem.at[0], recv_sem=in_sem.at[0],
+            device_id=plane(k // 4 - 3, k % 4), device_id_type=MESH,
+        ).start()
+        return carry
+
+    lax.fori_loop(0, 31, ship, 0)
+    pltpu.make_async_remote_copy(
+        src_ref=send.at[pl.ds(0, 31)], dst_ref=recv.at[tp, pl.ds(0, 31)], send_sem=out_sem.at[0],
+        recv_sem=in_sem.at[0], device_id=sibling, device_id_type=MESH,
+    ).wait()
+    swap = pltpu.make_async_remote_copy(
+        src_ref=recv.at[tp], dst_ref=recv.at[tp], send_sem=swap_sem.at[0], recv_sem=swap_sem.at[1],
+        device_id=sibling, device_id_type=MESH,
+    )
+    swap.start()
+    for load in loads:
+        load.wait()
+    swap.wait()
+
+    low = recv[0].reshape(SLOTS * SLAB, HALF)
+    high = recv[1].reshape(SLOTS * SLAB, HALF)
+
+    def proj(g):
+        return jnp.dot(low, wgu[g, :HALF, :], preferred_element_type=jnp.float32) + jnp.dot(
+            high, wgu[g, HALF:, :], preferred_element_type=jnp.float32
+        )
+
+    gate = proj(0)
+    up = proj(1)
+    hidden = (gate / (1.0 + jnp.exp(-gate)) * up).astype(jnp.bfloat16)
+    pair_send[...] = jnp.dot(hidden, wdn[:, theirs], preferred_element_type=jnp.float32).astype(jnp.bfloat16)
+    pair = pltpu.make_async_remote_copy(
+        src_ref=pair_send, dst_ref=pair_recv, send_sem=swap_sem.at[2], recv_sem=swap_sem.at[3],
+        device_id=sibling, device_id_type=MESH,
+    )
+    pair.start()
+    part = jnp.dot(hidden, wdn[:, mine], preferred_element_type=jnp.float32)
+    pair.wait()
+    total = (part + pair_recv[...].astype(jnp.float32)).astype(jnp.bfloat16)
+    back_send[...] = total.reshape(SLOTS, SLAB, HALF)
+    back_recv[OWN_SLOT] = total[OWN_SLOT * SLAB : (OWN_SLOT + 1) * SLAB]
+
+    def home(i, carry):
+        k = i + (i + 20) // 32
+        pltpu.make_async_remote_copy(
+            src_ref=back_send.at[k], dst_ref=back_recv.at[k], send_sem=out_sem.at[1], recv_sem=in_sem.at[1],
+            device_id=plane(3 - k // 4, 4 - k % 4), device_id_type=MESH,
+        ).start()
+        return carry
+
+    lax.fori_loop(0, 31, home, 0)
+    pltpu.make_async_remote_copy(
+        src_ref=back_send.at[pl.ds(0, 31)], dst_ref=back_recv.at[pl.ds(0, 31)], send_sem=out_sem.at[1],
+        recv_sem=in_sem.at[1], device_id=sibling, device_id_type=MESH,
+    ).wait()
+    got = back_recv[...].reshape(SLOTS * SLAB, HALF)
+    w_high = weighed.astype(jnp.bfloat16)
+    w_low = (weighed - w_high.astype(jnp.float32)).astype(jnp.bfloat16)
+    dims = (((0,), (0,)), ((), ()))
+    mixed = lax.dot_general(w_high, got, dims, preferred_element_type=jnp.float32) + lax.dot_general(
+        w_low, got, dims, preferred_element_type=jnp.float32
+    )
+    fin_send[...] = mixed.astype(jnp.bfloat16)
+    last = pltpu.make_async_remote_copy(
+        src_ref=fin_send, dst_ref=fin_recv, send_sem=swap_sem.at[4], recv_sem=swap_sem.at[5],
+        device_id=sibling, device_id_type=MESH,
+    )
+    last.start()
+    out_ref[:, mine] = mixed.astype(jnp.bfloat16)
+    last.wait()
+    out_ref[:, theirs] = fin_recv[...]
+
+
+def moe(hidden_in, routes, route_weight, w_gateup, w_down):
+    bf = jnp.bfloat16
+    vmem = pl.BlockSpec(memory_space=pltpu.VMEM)
+    hbm = pl.BlockSpec(memory_space=pl.ANY)
+    return pl.pallas_call(
+        moe_kernel,
+        out_shape=jax.ShapeDtypeStruct(hidden_in.shape, bf),
+        in_specs=[vmem, vmem, vmem, hbm, hbm],
+        out_specs=vmem,
+        scratch_shapes=[
+            pltpu.VMEM((2, D_MODEL, 256), bf),
+            pltpu.VMEM((256, D_MODEL), bf),
+            pltpu.VMEM((SLOTS, SLAB, HALF), bf),
+            pltpu.VMEM((2, SLOTS, SLAB, HALF), bf),
+            pltpu.VMEM((SLOTS * SLAB, HALF), bf),
+            pltpu.VMEM((SLOTS * SLAB, HALF), bf),
+            pltpu.VMEM((SLOTS, SLAB, HALF), bf),
+            pltpu.VMEM((SLOTS, SLAB, HALF), bf),
+            pltpu.VMEM((16, HALF), bf),
+            pltpu.VMEM((16, HALF), bf),
+            pltpu.SemaphoreType.DMA((2,)),
+            pltpu.SemaphoreType.DMA((2,)),
+            pltpu.SemaphoreType.DMA((2,)),
+            pltpu.SemaphoreType.DMA((6,)),
+        ],
+        compiler_params=pltpu.CompilerParams(
+            collective_id=1, has_side_effects=True, vmem_limit_bytes=40 * 1024 * 1024
+        ),
+    )(hidden_in, routes.T, route_weight.T, w_gateup[0].transpose(1, 0, 2), w_down[0])
 
 
 def local(
@@ -178,44 +349,7 @@
     )
     attended = lax.psum(head_terms.astype(jnp.bfloat16), "tp")
     hidden_in = rms_norm(tokens.astype(jnp.float32) + residual_scale * attended.astype(jnp.float32))
-    top_count = routes.shape[1]
-    expert_total = EXPERTS
-    local_experts = w_gateup.shape[0]
-    capacity = max(2, 3 * row_count * top_count // (2 * expert_total))
-    flat_route = routes.reshape(-1)
-    choose_map = (flat_route[:, None] == jnp.arange(expert_total, dtype=jnp.int32)[None, :]).astype(
-        jnp.int32
-    )
-    earlier_count = jnp.sum((jnp.cumsum(choose_map, 0) - choose_map) * choose_map, 1)
-    slot_index = flat_route * capacity + earlier_count
-    source_row = jnp.arange(flat_route.shape[0], dtype=jnp.int32) // top_count
-    outgoing = (
-        jnp.zeros((expert_total * capacity, model_width), jnp.bfloat16)
-        .at[slot_index]
-        .set(hidden_in[source_row])
-    )
-    outgoing = outgoing.reshape(expert_total // local_experts, local_experts, capacity, model_width)
-    gate_up = jnp.einsum(
-        "sxcd,xdgf->sxcgf",
-        lax.all_to_all(outgoing, "expert", split_axis=0, concat_axis=0, tiled=True),
-        w_gateup,
-        preferred_element_type=jnp.float32,
-    )
-    expert_hidden = (jax.nn.silu(gate_up[:, :, :, 0, :]) * gate_up[:, :, :, 1, :]).astype(
-        jnp.bfloat16
-    )
-    partial_out = jnp.einsum(
-        "sxcf,xfd->sxcd", expert_hidden, w_down, preferred_element_type=jnp.float32
-    )
-    summed = lax.psum(partial_out.astype(jnp.bfloat16), "tp")
-    sent_home = lax.all_to_all(summed, "expert", split_axis=0, concat_axis=0, tiled=True)
-    column_width = sent_home.shape[-1]
-    picked = sent_home.reshape(expert_total * capacity, column_width)[slot_index].reshape(
-        row_count, top_count, column_width
-    )
-    expert_mix = jnp.sum(route_weight[:, :, None] * picked.astype(jnp.float32), 1).astype(
-        jnp.bfloat16
-    )
+    expert_mix = moe(hidden_in, routes, route_weight, w_gateup, w_down)
     leaf_pick = (jnp.arange(tree_size, dtype=jnp.int32)[None, :] == accepted_leaf[:, None]).astype(
         jnp.float32
     )

time: 712 us -> 624 us (0.88)
  blocking collectives: 447 us -> 384 us
  waiting for transfers between devices: 159 us -> 106 us
  Pallas kernels: 0 us -> 38.9 us
  starting transfers between devices: 47.7 us -> 30.5 us
    all_to_all x1 -> x0, blocking collectives: 42.6 us -> none  [local(): lax.all_to_all(outgoing, 'expert', split_axis=0, concat_axis=0, tiled=True)]
    psum x1 -> x0, waiting for transfers between devices: 40.7 us -> none  [local(): summed = lax.psum(partial_out.astype(jnp.bfloat16), 'tp')]
    pallas_call x0 -> x1, Pallas kernels: none -> 38.9 us  [moe(): pl.pallas_call(moe_kernel, out_shape=jax.ShapeDtypeStruct(hidden_in.shape...]
    all_to_all x1 -> x0, waiting for transfers between devices: 37 us -> none  [local(): lax.all_to_all(summed, 'expert', split_axis=0, concat_axis=0, tiled=True)]
    ppermute x14, waiting for transfers between devices: 80.9 us -> 106 us  [passed_along(): return lax.ppermute(value, axis, pairs)]
    all_to_all x1 -> x0, starting transfers between devices: 11.5 us -> none  [local(): lax.all_to_all(summed, 'expert', split_axis=0, concat_axis=0, tiled=True)]
    psum x1, blocking collectives: 50.6 us -> 40 us  [local(): attended = lax.psum(head_terms.astype(jnp.bfloat16), 'tp')]
    ppermute x14, local copies, waits for them, and re-layouts: 8.13 us -> 16.7 us  [passed_along(): return lax.ppermute(value, axis, pairs)]
  transfers between devices with their start and end apart: 18 -> 16, of which waited for: 7 -> 8; matrix products, arithmetic and copies ran while one was open for 4% -> 6% of each run, Pallas kernels for 0% -> 0%
where the time goes in v1:
time: 624 us; the launch traced here: 617 us
  blocking collectives  384 us (62%)
  waiting for transfers between devices  106 us (17%)
  Pallas kernels  38.9 us (6%)
  starting transfers between devices  30.5 us (5%)
  local copies, waits for them, and re-layouts  19.9 us (3%)
  matrix products  15.9 us (3%)
  between operations  15.2 us (2%)
    all_gather x1, blocking collectives, local(): lax.all_gather(w_key, 'expert', axis=0, tiled=True)  118 us
    ppermute x14, waiting for transfers between devices, passed_along(): return lax.ppermute(value, axis, pairs)  106 us
    all_gather x1, blocking collectives, local(): lax.all_gather(w_value, 'expert', axis=0, tiled=True)  105 us
    all_gather x1, blocking collectives, local(): lax.all_gather(key_rows.reshape(req_count, part_size, kv_cols), 'blk', ax...  64.4 us
    all_gather x1, blocking collectives, local(): lax.all_gather(value_rows.reshape(req_count, part_size, kv_cols), 'blk',...  57.1 us
    psum x1, blocking collectives, local(): attended = lax.psum(head_terms.astype(jnp.bfloat16), 'tp')  40 us
    pallas_call x1, Pallas kernels, moe(): pl.pallas_call(moe_kernel, out_shape=jax.ShapeDtypeStruct(hidden_in.shape...  38.9 us
    ppermute x14, starting transfers between devices, passed_along(): return lax.ppermute(value, axis, pairs)  30.4 us
  transfers between devices with their start and end apart: 16, of which 8 were waited for; matrix products, arithmetic and copies ran while one was open for 6% of the time, Pallas kernels for 0%

profile of v1, /device:TPU:1, one launch (start us, length us, event | category | flops | bytes accessed | tf_op | source)
XLA Modules:
  0.0 617.2 jit_solution(506357579484750667)
XLA Ops:
  8.0 4.0 collective-permute-start
  12.0 3.2 collective-permute-start.1
  21.0 118.0 %all_gather.20 = bf16[1536,256]{1,0:T(8,128)(2,1)S(1)} all-gather(bf16[48,256]{1,0:T(8,128)(2,1)} %param.16), channel_id=1, replica_groups=mesh['blk'=8,'expert'=32,'tp'=2] {'expert'}, dimensions={0}, use_global_device_ids=true | all-gather | bytes 811008 | tf_op jit(solution)/shard_map/all_gather | solution.py:296
  139.7 64.4 %all_gather.21 = bf16[2,64,256]{2,1,0:T(8,128)(2,1)S(1)} all-gather(bf16[2,8,256]{2,1,0:T(8,128)(2,1)S(1)} %convert_element_type.163), channel_id=1, replica_groups=mesh['blk'=8,'expert'=32,'tp'=2] {'blk'}, dimensions={1}, use_global_device_ids=true | all-gather | bytes 73728 | tf_op jit(solution)/shard_map/all_gather | solution.py:312
  204.1 104.8 %all_gather.18 = bf16[1536,256]{1,0:T(8,128)(2,1)S(1)} all-gather(bf16[48,256]{1,0:T(8,128)(2,1)S(1)} %copy-done.26), channel_id=1, replica_groups=mesh['blk'=8,'expert'=32,'tp'=2] {'expert'}, dimensions={0}, use_global_device_ids=true | all-gather | bytes 811008 | tf_op jit(solution)/shard_map/all_gather | solution.py:301
  309.1 57.1 %all_gather.19 = bf16[2,64,256]{2,1,0:T(8,128)(2,1)S(1)} all-gather(bf16[2,8,256]{2,1,0:T(8,128)(2,1)S(1)} %fusion.62), channel_id=1, replica_groups=mesh['blk'=8,'expert'=32,'tp'=2] {'blk'}, dimensions={1}, use_global_device_ids=true | all-gather | bytes 73728 | tf_op jit(solution)/shard_map/all_gather | solution.py:313
  367.4 2.2 collective-permute-start.2
  369.5 1.9 collective-permute-start.3
  372.5 12.9 %collective-permute-done.2 = bf16[2,128,256]{2,1,0:T(8,128)(2,1)S(1)} collective-permute-done((bf16[2,128,256]{2,1,0:T(8,128)(2,1)S(1)}, bf16[2,128,256]{2,1,0:T(8,128)(2,1)S(1)}, u32[]{:S(2)}, u32[]{:S(2)}) %collective-permute-start.2) | collective-permute-done | bytes 131104 | tf_op jit(solution)/shard_map/ppermute | solution.py:20
  385.3 1.9 collective-permute-start.4
  387.3 1.9 collective-permute-start.5
  389.2 22.0 %collective-permute-done.4 = bf16[2,128,256]{2,1,0:T(8,128)(2,1)S(1)} collective-permute-done((bf16[2,128,256]{2,1,0:T(8,128)(2,1)S(1)}, bf16[2,128,256]{2,1,0:T(8,128)(2,1)S(1)}, u32[]{:S(2)}, u32[]{:S(2)}) %collective-permute-start.4) | collective-permute-done | bytes 131104 | tf_op jit(solution)/shard_map/ppermute | solution.py:20
  411.2 1.9 collective-permute-start.6
  413.1 1.9 collective-permute-start.7
  415.1 25.0 %collective-permute-done.6 = bf16[2,128,256]{2,1,0:T(8,128)(2,1)S(1)} collective-permute-done((bf16[2,128,256]{2,1,0:T(8,128)(2,1)S(1)}, bf16[2,128,256]{2,1,0:T(8,128)(2,1)S(1)}, u32[]{:S(2)}, u32[]{:S(2)}) %collective-permute-start.6) | collective-permute-done | bytes 131104 | tf_op jit(solution)/shard_map/ppermute | solution.py:20
  440.2 1.9 collective-permute-start.8
  443.0 1.9 collective-permute-start.9
  445.0 20.6 %collective-permute-done.8 = bf16[2,128,256]{2,1,0:T(8,128)(2,1)S(1)} collective-permute-done((bf16[2,128,256]{2,1,0:T(8,128)(2,1)S(1)}, bf16[2,128,256]{2,1,0:T(8,128)(2,1)S(1)}, u32[]{:S(2)}, u32[]{:S(2)}) %collective-permute-start.8) | collective-permute-done | bytes 131104 | tf_op jit(solution)/shard_map/ppermute | solution.py:20
  465.6 1.9 collective-permute-start.10
  468.6 1.9 collective-permute-start.11
  470.5 22.2 %collective-permute-done.10 = bf16[2,128,256]{2,1,0:T(8,128)(2,1)} collective-permute-done((bf16[2,128,256]{2,1,0:T(8,128)(2,1)S(1)}, bf16[2,128,256]{2,1,0:T(8,128)(2,1)}, u32[]{:S(2)}, u32[]{:S(2)}) %collective-permute-start.10) | collective-permute-done | bytes 131104 | tf_op jit(solution)/shard_map/ppermute | solution.py:20
  492.7 1.9 collective-permute-start.12
  494.6 1.1 collective-permute-done.11
  495.7 1.9 collective-permute-start.13
  501.4 1.7 copy.46
  504.1 1.7 copy.48
  506.8 1.7 copy.50
  509.5 1.7 copy.52
  517.2 2.1 fusion.202
  528.2 2.4 convolution_convert_fusion
  530.6 40.0 %psum.7 = bf16[16,1536]{1,0:T(8,128)(2,1)S(1)} all-reduce(bf16[16,1536]{1,0:T(8,128)(2,1)S(1)} %convolution_convert_fusion), channel_id=1, replica_groups=mesh['blk'=8,'expert'=32,'tp'=2] {'tp'}, use_global_device_ids=true, to_apply=%region_20.21 | all-reduce | flops 24576 | bytes 98304 | tf_op jit(solution)/shard_map/psum | solution.py:350
  570.9 38.9 %shard_map.165 = bf16[16,1536]{1,0:T(8,128)(2,1)S(1)} custom-call(bf16[16,1536]{1,0:T(8,128)(2,1)S(1)} %multiply_convert_fusion.hid_ref, s32[8,16]{1,0:T(8,128)S(1)} %bitcast.230, f32[8,16]{1,0:T(8,128)S(1)} %bitcast.231, bf16[2,1536,256]{2,1,0:T(8,128)(2,1)S(1)} %bitcast.228, bf16[256,1536]{1,0:T(8,128)(2,1)S(1)} %bitcast.229), custom_call_target="tpu_custom_call" | custom-call | tf_op jit(solution)/shard_map/pallas_call | solution.py:227
  (182 shorter events, 33.6 us)
Async XLA Ops:
  7.2 131.8 %copy-start.3 = (bf16[16,1536]{1,0:T(8,128)(2,1)S(1)}, bf16[16,1536]{1,0:T(8,128)(2,1)}, u32[]{:S(2)}) copy-start(bf16[16,1536]{1,0:T(8,128)(2,1)} %param.14) | copy-start | bytes 147460
  7.2 196.9 %copy-start.26 = (bf16[48,256]{1,0:T(8,128)(2,1)S(1)}, bf16[48,256]{1,0:T(8,128)(2,1)}, u32[]{:S(2)}) copy-start(bf16[48,256]{1,0:T(8,128)(2,1)} %param.17) | copy-start | bytes 73732
  7.2 510.0 %all-gather.3.cloned.1.call-start = ((), (), s32[]{:S(2)}) async-start(), calls=%async_computation | async-start | bytes 2433024 | tf_op jit(solution)/shard_map/all_gather | solution.py:291
  7.9 520.3 %all-gather.5.cloned.1.call-start = ((), (), s32[]{:S(2)}) async-start(), calls=%async_computation.1 | async-start | bytes 2433024 | tf_op jit(solution)/shard_map/all_gather | solution.py:347
  8.0 359.4 %collective-permute-start = (bf16[2,128,256]{2,1,0:T(8,128)(2,1)}, bf16[2,128,256]{2,1,0:T(8,128)(2,1)S(1)}, u32[]{:S(2)}, u32[]{:S(2)}) collective-permute-start(bf16[2,128,256]{2,1,0:T(8,128)(2,1)} %param.19), channel_id=1, source_target_pairs={{0,64},{64,128},{128,192},{192,256},{256,320},{320,384},{384,448},... | collective-permute-start | bytes 393224 | tf_op jit(solution)/shard_map/ppermute | solution.py:20
  12.0 357.5 %collective-permute-start.1 = (bf16[2,128,256]{2,1,0:T(8,128)(2,1)}, bf16[2,128,256]{2,1,0:T(8,128)(2,1)S(1)}, u32[]{:S(2)}, u32[]{:S(2)}) collective-permute-start(bf16[2,128,256]{2,1,0:T(8,128)(2,1)} %param.20), channel_id=1, source_target_pairs={{0,64},{64,128},{128,192},{192,256},{256,320},{320,384},{384,448},... | collective-permute-start | bytes 393224 | tf_op jit(solution)/shard_map/ppermute | solution.py:20
  16.6 349.8 %copy-start.7 = (bf16[2,128,256]{2,1,0:T(8,128)(2,1)S(1)}, bf16[2,128,256]{2,1,0:T(8,128)(2,1)}, u32[]{:S(2)}) copy-start(bf16[2,128,256]{2,1,0:T(8,128)(2,1)} %param.19) | copy-start | bytes 393220
  17.0 354.5 %copy-start.8 = (bf16[2,128,256]{2,1,0:T(8,128)(2,1)S(1)}, bf16[2,128,256]{2,1,0:T(8,128)(2,1)}, u32[]{:S(2)}) copy-start(bf16[2,128,256]{2,1,0:T(8,128)(2,1)} %param.20) | copy-start | bytes 393220
  18.4 479.2 %copy-start.32 = (s32[2]{0:T(128)S(1)}, s32[2]{0:T(128)}, u32[]{:S(2)}) copy-start(s32[2]{0:T(128)} %param.22) | copy-start | bytes 28
  20.9 287.9 %copy-start.33 = (f32[16]{0:T(128)}, f32[16]{0:T(128)S(1)}, u32[]{:S(2)}) copy-start(f32[16]{0:T(128)S(1)} %add_rsqrt_fusion.1) | copy-start | bytes 196
  138.9 361.2 %copy-start.4 = (bf16[1,1536,2,256]{3,2,1,0:T(2,128)(2,1)S(1)}, bf16[1,1536,2,256]{3,2,1,0:T(2,128)(2,1)}, u32[]{:S(2)}) copy-start(bf16[1,1536,2,256]{3,2,1,0:T(2,128)(2,1)} %param.26) | copy-start | bytes 4718596
  367.3 131.9 %copy-start.9 = (bf16[2,128,256]{2,1,0:T(8,128)(2,1)}, bf16[2,128,256]{2,1,0:T(8,128)(2,1)S(1)}, u32[]{:S(2)}) copy-start(bf16[2,128,256]{2,1,0:T(8,128)(2,1)S(1)} %collective-permute-done) | copy-start | bytes 393220
  367.4 18.0 %collective-permute-start.2 = (bf16[2,128,256]{2,1,0:T(8,128)(2,1)S(1)}, bf16[2,128,256]{2,1,0:T(8,128)(2,1)S(1)}, u32[]{:S(2)}, u32[]{:S(2)}) collective-permute-start(bf16[2,128,256]{2,1,0:T(8,128)(2,1)S(1)} %collective-permute-done), channel_id=1, source_target_pairs={{0,64},{64,128},{128,192},{192,256},{256,320},{320,384},{384,448},... | collective-permute-start | bytes 393224 | tf_op jit(solution)/shard_map/ppermute | solution.py:20
  369.5 129.8 %copy-start.10 = (bf16[2,128,256]{2,1,0:T(8,128)(2,1)}, bf16[2,128,256]{2,1,0:T(8,128)(2,1)S(1)}, u32[]{:S(2)}) copy-start(bf16[2,128,256]{2,1,0:T(8,128)(2,1)S(1)} %collective-permute-done.1) | copy-start | bytes 393220
  369.5 17.7 %collective-permute-start.3 = (bf16[2,128,256]{2,1,0:T(8,128)(2,1)S(1)}, bf16[2,128,256]{2,1,0:T(8,128)(2,1)S(1)}, u32[]{:S(2)}, u32[]{:S(2)}) collective-permute-start(bf16[2,128,256]{2,1,0:T(8,128)(2,1)S(1)} %collective-permute-done.1), channel_id=1, source_target_pairs={{0,64},{64,128},{128,192},{192,256},{256,320},{320,384},{384,448},... | collective-permute-start | bytes 393224 | tf_op jit(solution)/shard_map/ppermute | solution.py:20
  385.3 114.0 %copy-start.11 = (bf16[2,128,256]{2,1,0:T(8,128)(2,1)}, bf16[2,128,256]{2,1,0:T(8,128)(2,1)S(1)}, u32[]{:S(2)}) copy-start(bf16[2,128,256]{2,1,0:T(8,128)(2,1)S(1)} %collective-permute-done.2) | copy-start | bytes 393220
  385.3 25.9 %collective-permute-start.4 = (bf16[2,128,256]{2,1,0:T(8,128)(2,1)S(1)}, bf16[2,128,256]{2,1,0:T(8,128)(2,1)S(1)}, u32[]{:S(2)}, u32[]{:S(2)}) collective-permute-start(bf16[2,128,256]{2,1,0:T(8,128)(2,1)S(1)} %collective-permute-done.2), channel_id=1, source_target_pairs={{0,64},{64,128},{128,192},{192,256},{256,320},{320,384},{384,448},... | collective-permute-start | bytes 393224 | tf_op jit(solution)/shard_map/ppermute | solution.py:20
  387.2 112.1 %copy-start.12 = (bf16[2,128,256]{2,1,0:T(8,128)(2,1)}, bf16[2,128,256]{2,1,0:T(8,128)(2,1)S(1)}, u32[]{:S(2)}) copy-start(bf16[2,128,256]{2,1,0:T(8,128)(2,1)S(1)} %collective-permute-done.3) | copy-start | bytes 393220
  387.3 25.9 %collective-permute-start.5 = (bf16[2,128,256]{2,1,0:T(8,128)(2,1)S(1)}, bf16[2,128,256]{2,1,0:T(8,128)(2,1)S(1)}, u32[]{:S(2)}, u32[]{:S(2)}) collective-permute-start(bf16[2,128,256]{2,1,0:T(8,128)(2,1)S(1)} %collective-permute-done.3), channel_id=1, source_target_pairs={{0,64},{64,128},{128,192},{192,256},{256,320},{320,384},{384,448},... | collective-permute-start | bytes 393224 | tf_op jit(solution)/shard_map/ppermute | solution.py:20
  411.2 88.1 %copy-start.13 = (bf16[2,128,256]{2,1,0:T(8,128)(2,1)}, bf16[2,128,256]{2,1,0:T(8,128)(2,1)S(1)}, u32[]{:S(2)}) copy-start(bf16[2,128,256]{2,1,0:T(8,128)(2,1)S(1)} %collective-permute-done.4) | copy-start | bytes 393220
  411.2 29.0 %collective-permute-start.6 = (bf16[2,128,256]{2,1,0:T(8,128)(2,1)S(1)}, bf16[2,128,256]{2,1,0:T(8,128)(2,1)S(1)}, u32[]{:S(2)}, u32[]{:S(2)}) collective-permute-start(bf16[2,128,256]{2,1,0:T(8,128)(2,1)S(1)} %collective-permute-done.4), channel_id=1, source_target_pairs={{0,64},{64,128},{128,192},{192,256},{256,320},{320,384},{384,448},... | collective-permute-start | bytes 393224 | tf_op jit(solution)/shard_map/ppermute | solution.py:20
  413.1 86.2 %copy-start.14 = (bf16[2,128,256]{2,1,0:T(8,128)(2,1)}, bf16[2,128,256]{2,1,0:T(8,128)(2,1)S(1)}, u32[]{:S(2)}) copy-start(bf16[2,128,256]{2,1,0:T(8,128)(2,1)S(1)} %collective-permute-done.5) | copy-start | bytes 393220
  413.1 29.9 %collective-permute-start.7 = (bf16[2,128,256]{2,1,0:T(8,128)(2,1)S(1)}, bf16[2,128,256]{2,1,0:T(8,128)(2,1)S(1)}, u32[]{:S(2)}, u32[]{:S(2)}) collective-permute-start(bf16[2,128,256]{2,1,0:T(8,128)(2,1)S(1)} %collective-permute-done.5), channel_id=1, source_target_pairs={{0,64},{64,128},{128,192},{192,256},{256,320},{320,384},{384,448},... | collective-permute-start | bytes 393224 | tf_op jit(solution)/shard_map/ppermute | solution.py:20
  440.2 59.2 %copy-start.15 = (bf16[2,128,256]{2,1,0:T(8,128)(2,1)}, bf16[2,128,256]{2,1,0:T(8,128)(2,1)S(1)}, u32[]{:S(2)}) copy-start(bf16[2,128,256]{2,1,0:T(8,128)(2,1)S(1)} %collective-permute-done.6) | copy-start | bytes 393220
  440.2 25.4 %collective-permute-start.8 = (bf16[2,128,256]{2,1,0:T(8,128)(2,1)S(1)}, bf16[2,128,256]{2,1,0:T(8,128)(2,1)S(1)}, u32[]{:S(2)}, u32[]{:S(2)}) collective-permute-start(bf16[2,128,256]{2,1,0:T(8,128)(2,1)S(1)} %collective-permute-done.6), channel_id=1, source_target_pairs={{0,64},{64,128},{128,192},{192,256},{256,320},{320,384},{384,448},... | collective-permute-start | bytes 393224 | tf_op jit(solution)/shard_map/ppermute | solution.py:20
  443.0 56.3 %copy-start.16 = (bf16[2,128,256]{2,1,0:T(8,128)(2,1)}, bf16[2,128,256]{2,1,0:T(8,128)(2,1)S(1)}, u32[]{:S(2)}) copy-start(bf16[2,128,256]{2,1,0:T(8,128)(2,1)S(1)} %collective-permute-done.7) | copy-start | bytes 393220
  443.0 25.5 %collective-permute-start.9 = (bf16[2,128,256]{2,1,0:T(8,128)(2,1)S(1)}, bf16[2,128,256]{2,1,0:T(8,128)(2,1)S(1)}, u32[]{:S(2)}, u32[]{:S(2)}) collective-permute-start(bf16[2,128,256]{2,1,0:T(8,128)(2,1)S(1)} %collective-permute-done.7), channel_id=1, source_target_pairs={{0,64},{64,128},{128,192},{192,256},{256,320},{320,384},{384,448},... | collective-permute-start | bytes 393224 | tf_op jit(solution)/shard_map/ppermute | solution.py:20
  465.6 27.1 %collective-permute-start.10 = (bf16[2,128,256]{2,1,0:T(8,128)(2,1)S(1)}, bf16[2,128,256]{2,1,0:T(8,128)(2,1)}, u32[]{:S(2)}, u32[]{:S(2)}) collective-permute-start(bf16[2,128,256]{2,1,0:T(8,128)(2,1)S(1)} %collective-permute-done.8), channel_id=1, source_target_pairs={{0,64},{64,128},{128,192},{192,256},{256,320},{320,384},{384,448},... | collective-permute-start | bytes 393224 | tf_op jit(solution)/shard_map/ppermute | solution.py:20
  468.6 27.1 %collective-permute-start.11 = (bf16[2,128,256]{2,1,0:T(8,128)(2,1)S(1)}, bf16[2,128,256]{2,1,0:T(8,128)(2,1)}, u32[]{:S(2)}, u32[]{:S(2)}) collective-permute-start(bf16[2,128,256]{2,1,0:T(8,128)(2,1)S(1)} %collective-permute-done.9), channel_id=1, source_target_pairs={{0,64},{64,128},{128,192},{192,256},{256,320},{320,384},{384,448},... | collective-permute-start | bytes 393224 | tf_op jit(solution)/shard_map/ppermute | solution.py:20
  492.7 22.4 %collective-permute-start.12 = (bf16[2,128,256]{2,1,0:T(8,128)(2,1)}, bf16[2,128,256]{2,1,0:T(8,128)(2,1)}, u32[]{:S(2)}, u32[]{:S(2)}) collective-permute-start(bf16[2,128,256]{2,1,0:T(8,128)(2,1)} %collective-permute-done.10), channel_id=1, source_target_pairs={{0,64},{64,128},{128,192},{192,256},{256,320},{320,384},{384,448},... | collective-permute-start | bytes 393224 | tf_op jit(solution)/shard_map/ppermute | solution.py:20
  495.7 20.4 %collective-permute-start.13 = (bf16[2,128,256]{2,1,0:T(8,128)(2,1)}, bf16[2,128,256]{2,1,0:T(8,128)(2,1)}, u32[]{:S(2)}, u32[]{:S(2)}) collective-permute-start(bf16[2,128,256]{2,1,0:T(8,128)(2,1)} %collective-permute-done.11), channel_id=1, source_target_pairs={{0,64},{64,128},{128,192},{192,256},{256,320},{320,384},{384,448},... | collective-permute-start | bytes 393224 | tf_op jit(solution)/shard_map/ppermute | solution.py:20
  527.7 43.1 %copy-start = (bf16[1,256,1536]{2,1,0:T(8,128)(2,1)S(1)}, bf16[1,256,1536]{2,1,0:T(8,128)(2,1)}, u32[]{:S(2)}) copy-start(bf16[1,256,1536]{2,1,0:T(8,128)(2,1)} %param.27) | copy-start | bytes 2359300
  (19 other events, 270.7 us)
Sparse Core Ops, SparseCore 0:
  10.1 210.1 all-gather.2
  222.4 234.4 all-gather.4

commit v2 on v1

v2 whole, which is shorter than its diff:
```python
import jax
import jax.numpy as jnp
from jax import lax
from jax.experimental import pallas as pl
from jax.experimental.pallas import tpu as pltpu
from jax.sharding import PartitionSpec as P

score_scale = 0.015625
residual_scale = 0.22
masked_score = -1e30
D_MODEL = 1536
HALF = 768
SLOTS = 32
OWN_SLOT = 12
SLAB = 8
MESH = pl.DeviceIdType.MESH


def moe_kernel(hid_ref, routes_ref, weight_ref, wgu_hbm, wdn_hbm, out_ref, wgu, wdn, send, recv, pair_send,
               pair_recv, back_send, back_recv, fin_send, fin_recv, load_sem, out_sem, in_sem, swap_sem):
    blk = lax.axis_index("blk")
    exp = lax.axis_index("expert")
    tp = lax.axis_index("tp")
    z = (blk // 4) * 8 + exp // 4
    y = blk % 4
    x = exp % 4

    def plane(dz, dx):
        zz = (z + dz + 16) % 16
        return ((zz // 8) * 4 + y, (zz % 8) * 4 + (x + dx) % 4, tp)

    sibling = (blk, exp, 1 - tp)
    loads = [
        pltpu.make_async_copy(wgu_hbm, wgu, load_sem.at[0]),
        pltpu.make_async_copy(wdn_hbm, wdn, load_sem.at[1]),
    ]
    for load in loads:
        load.start()

    barrier = pltpu.get_barrier_semaphore()

    def greet(i, carry):
        q = i + (i + 20) // 36
        pl.semaphore_signal(barrier, inc=1, device_id=plane(q // 4 - 4, q % 4), device_id_type=MESH)
        return carry

    lax.fori_loop(0, 35, greet, 0)
    pl.semaphore_signal(barrier, inc=1, device_id=sibling, device_id_type=MESH)

    rows = hid_ref.shape[0]
    mine = pl.ds(pl.multiple_of(tp * HALF, HALF), HALF)
    theirs = pl.ds(pl.multiple_of((1 - tp) * HALF, HALF), HALF)
    slot = lax.broadcasted_iota(jnp.int32, (SLOTS * SLAB, rows), 0)
    kk = slot // SLAB
    cc = slot % SLAB
    expert_of = ((exp // 4 + kk // 4 + 5) % 8) * 4 + (x + kk % 4) % 4
    named = jnp.zeros((SLOTS * SLAB, rows), jnp.float32)
    weighed = jnp.zeros((SLOTS * SLAB, rows), jnp.float32)
    for t in range(8):
        hit = expert_of == routes_ref[t : t + 1, :]
        named = named + jnp.where(hit, 1.0, 0.0)
        weighed = weighed + jnp.where(hit, weight_ref[t : t + 1, :], 0.0)
    earlier = jnp.where(
        lax.broadcasted_iota(jnp.int32, (rows, rows), 0) < lax.broadcasted_iota(jnp.int32, (rows, rows), 1), 1.0, 0.0
    ).astype(jnp.bfloat16)
    rank = jnp.dot(named.astype(jnp.bfloat16), earlier, preferred_element_type=jnp.float32)
    chosen = jnp.where((named > 0.5) & (jnp.abs(rank - cc.astype(jnp.float32)) < 0.5), 1.0, 0.0)
    weighed = weighed * chosen
    packed = jnp.dot(chosen.astype(jnp.bfloat16), hid_ref[:, mine], preferred_element_type=jnp.float32)
    send[...] = packed.astype(jnp.bfloat16).reshape(SLOTS, SLAB, HALF)
    recv[tp, OWN_SLOT] = packed[OWN_SLOT * SLAB : (OWN_SLOT + 1) * SLAB].astype(jnp.bfloat16)
    pl.semaphore_wait(barrier, 36)

    def ship(i, carry):
        k = i + (i + 20) // 32
        pltpu.make_async_remote_copy(
            src_ref=send.at[k], dst_ref=recv.at[tp, k], send_sem=out_sem.at[0], recv_sem=in_sem.at[0],
            device_id=plane(k // 4 - 3, k % 4), device_id_type=MESH,
        ).start()
        return carry

    lax.fori_loop(0, 31, ship, 0)
    pltpu.make_async_remote_copy(
        src_ref=send.at[pl.ds(0, 31)], dst_ref=recv.at[tp, pl.ds(0, 31)], send_sem=out_sem.at[0],
        recv_sem=in_sem.at[0], device_id=sibling, device_id_type=MESH,
    ).wait()
    swap = pltpu.make_async_remote_copy(
        src_ref=recv.at[tp], dst_ref=recv.at[tp], send_sem=swap_sem.at[0], recv_sem=swap_sem.at[1],
        device_id=sibling, device_id_type=MESH,
    )
    swap.start()
    for load in loads:
        load.wait()
    swap.wait()

    low = recv[0].reshape(SLOTS * SLAB, HALF)
    high = recv[1].reshape(SLOTS * SLAB, HALF)

    def proj(g):
        return jnp.dot(low, wgu[g, :HALF, :], preferred_element_type=jnp.float32) + jnp.dot(
            high, wgu[g, HALF:, :], preferred_element_type=jnp.float32
        )

    gate = proj(0)
    up = proj(1)
    hidden = (gate / (1.0 + jnp.exp(-gate)) * up).astype(jnp.bfloat16)
    pair_send[...] = jnp.dot(hidden, wdn[:, theirs], preferred_element_type=jnp.float32).astype(jnp.bfloat16)
    pair = pltpu.make_async_remote_copy(
        src_ref=pair_send, dst_ref=pair_recv, send_sem=swap_sem.at[2], recv_sem=swap_sem.at[3],
        device_id=sibling, device_id_type=MESH,
    )
    pair.start()
    part = jnp.dot(hidden, wdn[:, mine], preferred_element_type=jnp.float32)
    pair.wait()
    total = (part + pair_recv[...].astype(jnp.float32)).astype(jnp.bfloat16)
    back_send[...] = total.reshape(SLOTS, SLAB, HALF)
    back_recv[OWN_SLOT] = total[OWN_SLOT * SLAB : (OWN_SLOT + 1) * SLAB]

    def home(i, carry):
        k = i + (i + 20) // 32
        pltpu.make_async_remote_copy(
            src_ref=back_send.at[k], dst_ref=back_recv.at[k], send_sem=out_sem.at[1], recv_sem=in_sem.at[1],
            device_id=plane(3 - k // 4, 4 - k % 4), device_id_type=MESH,
        ).start()
        return carry

    lax.fori_loop(0, 31, home, 0)
    pltpu.make_async_remote_copy(
        src_ref=back_send.at[pl.ds(0, 31)], dst_ref=back_recv.at[pl.ds(0, 31)], send_sem=out_sem.at[1],
        recv_sem=in_sem.at[1], device_id=sibling, device_id_type=MESH,
    ).wait()
    got = back_recv[...].reshape(SLOTS * SLAB, HALF)
    w_high = weighed.astype(jnp.bfloat16)
    w_low = (weighed - w_high.astype(jnp.float32)).astype(jnp.bfloat16)
    dims = (((0,), (0,)), ((), ()))
    mixed = lax.dot_general(w_high, got, dims, preferred_element_type=jnp.float32) + lax.dot_general(
        w_low, got, dims, preferred_element_type=jnp.float32
    )
    fin_send[...] = mixed.astype(jnp.bfloat16)
    last = pltpu.make_async_remote_copy(
        src_ref=fin_send, dst_ref=fin_recv, send_sem=swap_sem.at[4], recv_sem=swap_sem.at[5],
        device_id=sibling, device_id_type=MESH,
    )
    last.start()
    out_ref[:, mine] = mixed.astype(jnp.bfloat16)
    last.wait()
    out_ref[:, theirs] = fin_recv[...]


def moe(hidden_in, routes, route_weight, w_gateup, w_down):
    bf = jnp.bfloat16
    vmem = pl.BlockSpec(memory_space=pltpu.VMEM)
    hbm = pl.BlockSpec(memory_space=pl.ANY)
    return pl.pallas_call(
        moe_kernel,
        out_shape=jax.ShapeDtypeStruct(hidden_in.shape, bf),
        in_specs=[vmem, vmem, vmem, hbm, hbm],
        out_specs=vmem,
        scratch_shapes=[
            pltpu.VMEM((2, D_MODEL, 256), bf),
            pltpu.VMEM((256, D_MODEL), bf),
            pltpu.VMEM((SLOTS, SLAB, HALF), bf),
            pltpu.VMEM((2, SLOTS, SLAB, HALF), bf),
            pltpu.VMEM((SLOTS * SLAB, HALF), bf),
            pltpu.VMEM((SLOTS * SLAB, HALF), bf),
            pltpu.VMEM((SLOTS, SLAB, HALF), bf),
            pltpu.VMEM((SLOTS, SLAB, HALF), bf),
            pltpu.VMEM((16, HALF), bf),
            pltpu.VMEM((16, HALF), bf),
            pltpu.SemaphoreType.DMA((2,)),
            pltpu.SemaphoreType.DMA((2,)),
            pltpu.SemaphoreType.DMA((2,)),
            pltpu.SemaphoreType.DMA((6,)),
        ],
        compiler_params=pltpu.CompilerParams(
            collective_id=1, has_side_effects=True, vmem_limit_bytes=40 * 1024 * 1024
        ),
    )(hidden_in, routes.T, route_weight.T, w_gateup[0].transpose(1, 0, 2), w_down[0])


TREE = 64
ROWS = 128
CARRIED = 160


def attend_kernel(len_ref, leaf_ref, tok_ref, wq_ref, wk_ref, wv_ref, ck_ref, cv_ref, par_ref, wo_hbm, att_ref, hid_ref,
                  nk_ref, nv_ref, toks, slices, wall, wout, normed_ref, made, part_send, part_recv, stat_send, stat_recv,
                  pair_send, pair_recv, tok_out, tok_in, made_out, made_in, qa_out, qa_in, qb_out, qb_in, oa_out, oa_in,
                  ob_out, ob_in, part_sem, pair_sem, own_sem):
    f32, bf = jnp.float32, jnp.bfloat16
    blk = lax.axis_index("blk")
    exp = lax.axis_index("expert")
    tp = lax.axis_index("tp")
    hi = blk // 4
    y = blk % 4
    z = hi * 8 + exp // 4
    x = exp % 4
    partner = (1 - hi) * 4 + y

    def along_z(dz):
        zz = (z + dz + 16) % 16
        return ((zz // 8) * 4 + y, (zz % 8) * 4 + x, tp)

    def along_x(dx):
        return (blk, (exp // 4) * 4 + (x + dx) % 4, tp)

    def along_y(dy):
        return (hi * 4 + (y + dy) % 4, exp, tp)

    across = (partner, exp, tp)
    sibling = (blk, exp, 1 - tp)

    def source_row(slot):
        return ((z - (slot - 3) + 16) % 8) * 4 + x

    def remote(src, dst, ssem, rsem, device):
        return pltpu.make_async_remote_copy(
            src_ref=src, dst_ref=dst, send_sem=ssem, recv_sem=rsem, device_id=device, device_id_type=MESH
        )

    own_out = pltpu.make_async_copy(wo_hbm, wout.at[exp], own_sem.at[0])
    own_out.start()

    barrier = pltpu.get_barrier_semaphore()

    def greet_z(i, carry):
        pl.semaphore_signal(barrier, inc=1, device_id=along_z(i - 4 + (i + 4) // 8), device_id_type=MESH)
        return carry

    lax.fori_loop(0, 8, greet_z, 0)
    for d in range(1, 4):
        pl.semaphore_signal(barrier, inc=1, device_id=along_x(d), device_id_type=MESH)

    def greet_blk(i, carry):
        pl.semaphore_signal(barrier, inc=1, device_id=((blk + 1 + i) % 8, exp, tp), device_id_type=MESH)
        return carry

    lax.fori_loop(0, 7, greet_blk, 0)
    pl.semaphore_signal(barrier, inc=1, device_id=sibling, device_id_type=MESH)

    for b in range(8):
        if b < 6:
            slices[b, :, 0:128] = wq_ref[:, b * 128 : (b + 1) * 128]
        else:
            slices[b, :, 0:128] = wk_ref[:, (b - 6) * 128 : (b - 5) * 128]
        slices[b, :, 128:256] = wv_ref[:, (b // 4) * 128 : (b // 4 + 1) * 128]
    wall[exp] = slices[blk]
    toks[blk] = tok_ref[...]
    pl.semaphore_wait(barrier, 19)

    def share_start(buf, ssem, rsem):
        for d in range(1, 4):
            remote(buf.at[blk], buf.at[blk], ssem.at[d - 1], rsem.at[d - 1], along_y(d)).start()
        remote(buf.at[blk], buf.at[blk], ssem.at[3], rsem.at[3], across).start()

    def share_forward(buf, ssem, rsem):
        remote(buf.at[partner], buf.at[partner], ssem.at[3], rsem.at[3], across).wait_recv()
        for d in range(1, 4):
            remote(buf.at[partner], buf.at[partner], ssem.at[3 + d], rsem.at[3 + d], along_y(d)).start()

    def share_finish(buf, ssem, rsem):
        for d in range(1, 4):
            for half in range(2):
                remote(
                    buf.at[blk], buf.at[(hi + half) % 2 * 4 + (y + 4 - d) % 4], ssem.at[d - 1 + 4 * half],
                    rsem.at[d - 1 + 4 * half], across,
                ).wait_recv()

    def share_sent(buf, ssem, rsem):
        for s in range(7):
            remote(buf.at[blk], buf.at[blk], ssem.at[s], rsem.at[s], across).wait_send()

    def slot_of(i):
        return i + (i + 5) // 8

    share_start(toks, tok_out, tok_in)

    def weights_a(i, carry):
        slot = slot_of(i)
        to = along_z(slot - 3)
        remote(slices.at[to[0]], wall.at[exp], qa_out.at[0], qa_in.at[slot], to).start()
        return carry

    lax.fori_loop(0, 7, weights_a, 0)

    def pass_on(slot, buf, ssem, rsem):
        row = source_row(slot)
        for d in range(1, 4):
            remote(buf.at[row], buf.at[row], ssem.at[0], rsem.at[0], along_x(d)).start()

    pass_on(3, wall, qb_out, qb_in)

    def out_a(i, carry):
        slot = slot_of(i)
        remote(wo_hbm, wout.at[exp], oa_out.at[0], oa_in.at[slot], along_z(slot - 3)).start()
        return carry

    lax.fori_loop(0, 7, out_a, 0)

    lane = lax.broadcasted_iota(jnp.int32, (ROWS, 128), 1)
    line = lax.broadcasted_iota(jnp.int32, (ROWS, 128), 0)
    parent = par_ref[...]
    parent = jnp.where(parent >= 0, parent + 64 * (lax.broadcasted_iota(jnp.int32, (1, 128), 1) // 64), -1)
    eye = jnp.where(lane == line, 1.0, 0.0)
    upward = eye + jnp.where(line == parent, 1.0, 0.0)
    for doubling in range(6):
        short = upward.astype(bf)
        upward = jnp.minimum(upward + jnp.dot(short, short, preferred_element_type=f32), 1.0)
    upward_bf = upward.astype(bf)
    dims0 = (((0,), (0,)), ((), ()))
    reach = lax.dot_general(upward_bf, eye.astype(bf), dims0, preferred_element_type=f32)
    depth = lax.dot_general(upward_bf, jnp.ones((ROWS, 128), bf), dims0, preferred_element_type=f32) - 1.0
    len0 = len_ref[0].astype(f32)
    len1 = len_ref[1].astype(f32)
    place = depth + jnp.where(line < 64, len0, len1)
    rate = jnp.exp((lane % 32).astype(f32) * (-9.210340371976184 / 32.0))
    angle = place * rate
    cos = jnp.cos(angle)
    low_half = (lane % 64) < 32
    sin = jnp.where(low_half, -1.0, 1.0) * jnp.sin(angle)
    target = jnp.sum(upward, axis=0, keepdims=True) - 1.0 + jnp.where(lane[0:1] < 64, len0, len1)
    on_path = jnp.sum(
        jnp.where((line == leaf_ref[0]) | (line == leaf_ref[1] + 64), reach, 0.0), axis=0, keepdims=True
    )

    share_forward(toks, tok_out, tok_in)

    def weights_b(i, carry):
        slot = slot_of(i)
        row = source_row(slot)
        remote(wall.at[row], wall.at[row], qa_out.at[0], qa_in.at[slot], across).wait_recv()
        pass_on(slot, wall, qb_out, qb_in)
        return carry

    lax.fori_loop(0, 7, weights_b, 0)
    share_finish(toks, tok_out, tok_in)

    for r in range(2):
        rows = toks[:, r].reshape(TREE, D_MODEL).astype(f32)
        scale = lax.rsqrt(jnp.mean(rows * rows, axis=-1, keepdims=True) + 1e-06)
        normed_ref[r * TREE : (r + 1) * TREE, :] = (rows * scale).astype(bf)
    remote(wall.at[pl.ds(0, 24)], wall.at[pl.ds(0, 24)], qb_out.at[0], qb_in.at[0], across).wait_recv()
    w_first = wall[:, :, 0:128].reshape(D_MODEL, 128)
    w_second = wall[:, :, 128:256].reshape(D_MODEL, 128)
    first = jnp.dot(normed_ref[...], w_first, preferred_element_type=f32)
    turned = jnp.where(low_half, pltpu.roll(first, 96, 1), pltpu.roll(first, 32, 1))
    made[blk, 0:ROWS, :] = (first * cos + turned * sin).astype(bf)
    quarter = normed_ref[pl.ds(pl.multiple_of(y * 32, 32), 32), :]
    made[blk, ROWS:CARRIED, :] = jnp.dot(quarter, w_second, preferred_element_type=f32).astype(bf)

    share_start(made, made_out, made_in)

    own_out.wait()
    pass_on(3, wout, ob_out, ob_in)

    def out_b(i, carry):
        slot = slot_of(i)
        row = source_row(slot)
        remote(wout.at[row], wout.at[row], oa_out.at[0], oa_in.at[slot], across).wait_recv()
        pass_on(slot, wout, ob_out, ob_in)
        return carry

    share_forward(made, made_out, made_in)
    lax.fori_loop(0, 7, out_b, 0)
    share_finish(made, made_out, made_in)

    tree_k = [made[6 + c, 0:ROWS, :] for c in range(2)]
    tree_v = [jnp.concatenate([made[c * 4 + q, ROWS:CARRIED, :] for q in range(4)], axis=0) for c in range(2)]
    nt = (((1,), (1,)), ((), ()))
    left = lane < 64
    for r in range(2):
        length = len0 if r == 0 else len1
        sees = (lane[0:1] + blk * 128).astype(f32) < length
        tree_ok = (reach[r * TREE : (r + 1) * TREE] > 0.5) & (((lane[0:TREE] % 64) // 8) == blk)
        left64 = left[0:TREE]
        lane64 = lane[0:TREE]
        stat = jnp.zeros((TREE, 128), f32)
        tops = []
        for c in range(2):
            stack = []
            for head in range(6 * c, 6 * c + 6):
                block = made[head // 2, r * TREE : (r + 1) * TREE, :].astype(f32)
                side = (head // 3) % 2
                if side != head % 2:
                    block = pltpu.roll(block, 64, 1)
                stack.append(jnp.where(left64 if side == 0 else ~left64, block, 0.0).astype(bf))
            query = jnp.concatenate(stack, axis=0)
            cols = slice(c * 128, (c + 1) * 128)
            s_cache = lax.dot_general(query, ck_ref[r, :, cols], nt, preferred_element_type=f32) * score_scale
            s_tree = lax.dot_general(query, tree_k[c], nt, preferred_element_type=f32) * score_scale
            s_cache = jnp.where(sees, s_cache, masked_score).reshape(6, TREE, 128)
            s_tree = jnp.where(tree_ok, s_tree.reshape(6, TREE, 128), masked_score)
            peak = jnp.maximum(
                jnp.max(s_cache, axis=-1, keepdims=True), jnp.max(s_tree, axis=-1, keepdims=True)
            )
            p_cache = jnp.where(sees, jnp.exp(s_cache - peak), 0.0)
            p_tree = jnp.where(tree_ok, jnp.exp(s_tree - peak), 0.0)
            mass = jnp.sum(p_cache, axis=-1, keepdims=True) + jnp.sum(p_tree, axis=-1, keepdims=True)
            total = jnp.dot(
                p_cache.reshape(6 * TREE, 128).astype(bf), cv_ref[r, :, cols], preferred_element_type=f32
            ) + jnp.dot(p_tree.reshape(6 * TREE, 128).astype(bf), tree_v[c], preferred_element_type=f32)
            total = total.reshape(6, TREE, 128) / jnp.where(mass > 0.0, mass, 1.0)
            for n in range(6):
                head = 6 * c + n
                stat = jnp.where(lane64 == head, peak[n], stat)
                stat = jnp.where(lane64 == 64 + head, mass[n], stat)
                tops.append(total[n])
        for i in range(6):
            parts = []
            for u in range(2):
                head = 2 * i + u
                value = tops[head]
                if (head // 3) % 2 != u:
                    value = pltpu.roll(value, 64, 1)
                parts.append(value)
            joined = jnp.where(left64, parts[0], parts[1])
            part_send[:, r, :, i * 128 : (i + 1) * 128] = joined.astype(bf).reshape(8, 8, 128)
        stat_send[:, r, :, :] = stat.reshape(8, 8, 128)

    def parts_out(i, carry):
        to = (blk + 1 + i) % 8
        remote(part_send.at[to], part_recv.at[blk], part_sem.at[0], part_sem.at[1], (to, exp, tp)).start()
        remote(stat_send.at[to], stat_recv.at[blk], part_sem.at[2], part_sem.at[3], (to, exp, tp)).start()
        return carry

    lax.fori_loop(0, 7, parts_out, 0)
    part_recv[blk] = part_send[blk]
    stat_recv[blk] = stat_send[blk]

    for r in range(2):
        spot = (line + blk * 128).astype(f32)
        placing = jnp.where((spot == target) & (on_path > 0.5) & ((lane // 64) == r), 1.0, 0.0)
        written = jnp.max(placing, axis=-1, keepdims=True) > 0.5
        placing = placing.astype(bf)
        for c in range(2):
            cols = slice(c * 128, (c + 1) * 128)
            moved_k = jnp.dot(placing, tree_k[c], preferred_element_type=f32)
            nk_ref[r, :, cols] = jnp.where(written, moved_k, ck_ref[r, :, cols].astype(f32)).astype(bf)
            moved_v = jnp.dot(placing, tree_v[c], preferred_element_type=f32)
            nv_ref[r, :, cols] = jnp.where(written, moved_v, cv_ref[r, :, cols].astype(f32)).astype(bf)

    remote(part_send.at[pl.ds(0, 7)], part_recv.at[pl.ds(0, 7)], part_sem.at[0], part_sem.at[1], across).wait()
    remote(stat_send.at[pl.ds(0, 7)], stat_recv.at[pl.ds(0, 7)], part_sem.at[2], part_sem.at[3], across).wait()
    stats = stat_recv[...].reshape(8, 16, 128)
    masses = pltpu.roll(stats.reshape(ROWS, 128), 64, 1).reshape(8, 16, 128)
    peak = jnp.max(stats, axis=0, keepdims=True)
    share = jnp.where(lane[0:16] < 12, masses * jnp.exp(stats - peak), 0.0)
    whole = jnp.sum(share, axis=0, keepdims=True)
    share = (share / jnp.where(whole > 0.0, whole, 1.0)).reshape(ROWS, 128)
    spread = jnp.where(
        lax.broadcasted_iota(jnp.int32, (128, HALF), 1) // 64 == lax.broadcasted_iota(jnp.int32, (128, HALF), 0), 1.0, 0.0
    ).astype(bf)
    share_high = share.astype(bf)
    share_low = (share - share_high.astype(f32)).astype(bf)
    factor = jnp.dot(share_high, spread, preferred_element_type=f32) + jnp.dot(
        share_low, spread, preferred_element_type=f32
    )
    context = jnp.sum(
        factor.reshape(8, 16, HALF) * part_recv[...].reshape(8, 16, HALF).astype(f32), axis=0
    ).astype(bf)
    remote(wout.at[pl.ds(0, 24)], wout.at[pl.ds(0, 24)], ob_out.at[0], ob_in.at[0], across).wait_recv()
    terms = lax.dot_general(context, wout[...].reshape(D_MODEL, HALF), nt, preferred_element_type=f32).astype(bf)
    pair_send[...] = terms
    pair = remote(pair_send, pair_recv, pair_sem.at[0], pair_sem.at[1], sibling)
    pair.start()
    pair.wait()
    attended = (terms.astype(f32) + pair_recv[...].astype(f32)).astype(bf)
    att_ref[...] = attended
    mixed = tok_ref[...].reshape(16, D_MODEL).astype(f32) + residual_scale * attended.astype(f32)
    scale = lax.rsqrt(jnp.mean(mixed * mixed, axis=-1, keepdims=True) + 1e-06)
    hid_ref[...] = (mixed * scale).astype(bf)

    share_sent(toks, tok_out, tok_in)
    share_sent(made, made_out, made_in)
    remote(wall.at[pl.ds(0, 7)], wall.at[pl.ds(0, 7)], qa_out.at[0], qb_in.at[0], across).wait_send()
    remote(wall.at[pl.ds(0, 24)], wall.at[pl.ds(0, 24)], qb_out.at[0], qb_in.at[0], across).wait_send()
    remote(wout.at[pl.ds(0, 7)], wout.at[pl.ds(0, 7)], oa_out.at[0], ob_in.at[0], across).wait_send()
    remote(wout.at[pl.ds(0, 24)], wout.at[pl.ds(0, 24)], ob_out.at[0], ob_in.at[0], across).wait_send()


def attend(tokens, w_query, w_key, w_value, w_out, cache_keys, cache_values, parents, lengths, accepted_leaf):
    bf = jnp.bfloat16
    vmem = pl.BlockSpec(memory_space=pltpu.VMEM)
    smem = pl.BlockSpec(memory_space=pltpu.SMEM)
    dma = pltpu.SemaphoreType.DMA
    return pl.pallas_call(
        attend_kernel,
        out_shape=(
            jax.ShapeDtypeStruct(tokens.shape, bf),
            jax.ShapeDtypeStruct(tokens.shape, bf),
            jax.ShapeDtypeStruct(cache_keys.shape, bf),
            jax.ShapeDtypeStruct(cache_values.shape, bf),
        ),
        in_specs=[smem, smem] + [vmem] * 7 + [pl.BlockSpec(memory_space=pl.ANY)],
        out_specs=(vmem,) * 4,
        scratch_shapes=[
            pltpu.VMEM((8, 2, 8, D_MODEL), bf),
            pltpu.VMEM((8, 48, 256), bf),
            pltpu.VMEM((32, 48, 256), bf),
            pltpu.VMEM((32, 48, HALF), bf),
            pltpu.VMEM((ROWS, D_MODEL), bf),
            pltpu.VMEM((8, CARRIED, 128), bf),
            pltpu.VMEM((8, 2, 8, HALF), bf),
            pltpu.VMEM((8, 2, 8, HALF), bf),
            pltpu.VMEM((8, 2, 8, 128), jnp.float32),
            pltpu.VMEM((8, 2, 8, 128), jnp.float32),
            pltpu.VMEM((16, D_MODEL), bf),
            pltpu.VMEM((16, D_MODEL), bf),
            dma((7,)), dma((7,)), dma((7,)), dma((7,)),
            dma((1,)), dma((8,)), dma((1,)), dma((1,)),
            dma((1,)), dma((8,)), dma((1,)), dma((1,)),
            dma((4,)), dma((2,)), dma((1,)),
        ],
        compiler_params=pltpu.CompilerParams(
            collective_id=2, has_side_effects=True, vmem_limit_bytes=40 * 1024 * 1024
        ),
    )(
        lengths, accepted_leaf, tokens.reshape(2, 8, D_MODEL), w_query, w_key, w_value, cache_keys, cache_values,
        parents.reshape(1, 128), w_out.T,
    )


def local(tokens, w_query, w_key, w_value, w_out, cache_keys, cache_values, parents, lengths, accepted_leaf, routes,
          route_weight, w_gateup, w_down):
    attended, hidden_in, new_keys, new_values = attend(
        tokens, w_query, w_key, w_value, w_out, cache_keys, cache_values, parents, lengths, accepted_leaf
    )
    expert_mix = moe(hidden_in, routes, route_weight, w_gateup, w_down)
    return (attended, expert_mix, new_keys, new_values)


def solution(mesh):
    in_specs = (
        P(("blk", "expert"), None),
        P("expert", "tp"),
        P("expert", "tp"),
        P("expert", "tp"),
        P("tp", "expert"),
        P("expert", "blk", "tp"),
        P("expert", "blk", "tp"),
        P("expert", None),
        P("expert"),
        P("expert"),
        P(("blk", "expert"), None),
        P(("blk", "expert"), None),
        P("expert", None, None, "tp"),
        P("expert", "tp", None),
    )
    out_specs = (
        P(("blk", "expert"), None),
        P(("blk", "expert"), None),
        P("expert", "blk", "tp"),
        P("expert", "blk", "tp"),
    )
    return jax.shard_map(local, mesh=mesh, in_specs=in_specs, out_specs=out_specs, check_vma=False)
```

time: 624 us -> 131 us (0.21)
  the two profiles are of different devices: /device:TPU:1 before, /device:TPU:41 now
where the time goes in v2:
time: 131 us
  Pallas kernels  118 us (90%)
  local copies, waits for them, and re-layouts  12.2 us (9%)
    pallas_call x1, Pallas kernels, attend(): pl.pallas_call(attend_kernel, out_shape=(jax.ShapeDtypeStruct(tokens.shap...  67.9 us
    pallas_call x1, Pallas kernels, moe(): pl.pallas_call(moe_kernel, out_shape=jax.ShapeDtypeStruct(hidden_in.shape...  50.1 us
    unnamed x29, local copies, waits for them, and re-layouts  11.4 us

profile of v2, /device:TPU:41, one launch (start us, length us, event | category | flops | bytes accessed | tf_op | source)
XLA Modules:
  0.0 130.9 jit_solution(16709657544990736525)
XLA Ops:
  0.6 0.8 reshape.15.par_ref
  1.4 0.0 copy-start.1
  1.4 0.9 copy-done.1
  2.3 0.0 copy-start.2
  2.3 0.9 copy-done.2
  3.2 0.0 copy-start.3
  3.2 0.9 copy-done.3
  4.1 0.0 copy-start.4
  4.1 0.9 copy-done.4
  5.0 0.0 copy-start.5
  5.0 0.8 copy-done.5
  5.8 0.0 copy-start.6
  5.8 0.7 copy-done.6
  6.5 0.0 copy-start.7
  6.5 0.7 copy-done.7
  7.2 0.0 copy-start.10
  7.2 0.7 copy-done.10
  7.9 0.0 copy-start.11
  7.9 0.7 copy-done.11
  8.6 67.9 %shard_map.165 = (bf16[16,1536]{1,0:T(8,128)(2,1)S(1)}, bf16[16,1536]{1,0:T(8,128)(2,1)S(1)}, bf16[2,128,256]{2,1,0:T(8,128)(2,1)S(1)}, bf16[2,128,256]{2,1,0:T(8,128)(2,1)S(1)}) custom-call(s32[2]{0:T(128)S(1)} %copy-done.10, s32[2]{0:T(128)S(1)} %copy-done.11, bf16[2,8,1536]{2,1,0:T(8,128)(2,1)S(1)} %bitcast.13, bf16[48,768]{1,0:T(8,128)(2,1)S(1)} %copy-done.3, ...), custom_call_target="tpu_custom_call" | custom-call | tf_op jit(solution)/shard_map/pallas_call | solution.py:486
  76.5 0.0 copy-start
  76.5 0.0 copy-start.8
  76.5 0.0 copy-start.9
  76.5 1.7 %copy.20 = bf16[1,1536,2,256]{3,1,2,0:T(8,128)(2,1)S(1)} copy(bf16[1,1536,2,256]{3,2,1,0:T(2,128)(2,1)} %param.26) | data formatting | bytes 3145728 | tf_op args[12]
  78.2 0.0 copy-done
  78.2 0.0 copy-done.8
  78.3 0.0 copy-done.9
  78.3 50.1 %shard_map.166 = bf16[16,1536]{1,0:T(8,128)(2,1)S(1)} custom-call(bf16[16,1536]{1,0:T(8,128)(2,1)S(1)} %get-tuple-element.9.hid_ref, s32[8,16]{1,0:T(8,128)S(1)} %bitcast.14, f32[8,16]{1,0:T(8,128)S(1)} %bitcast.15, bf16[2,1536,256]{2,1,0:T(8,128)(2,1)S(1)} %bitcast.10, bf16[256,1536]{1,0:T(8,128)(2,1)S(1)} %bitcast.11), custom_call_target="tpu_custom_call" | custom-call | tf_op jit(solution)/shard_map/pallas_call | solution.py:154
  128.4 0.6 copy.25
  129.0 0.6 copy.26
  129.6 0.7 copy.27
  130.3 0.7 copy.28
Async XLA Ops:
  1.4 0.9 copy-start.1
  2.3 0.9 copy-start.2
  3.2 0.9 copy-start.3
  4.1 0.9 copy-start.4
  5.0 0.8 copy-start.5
  5.8 0.7 copy-start.6
  6.5 0.7 copy-start.7
  7.2 0.7 copy-start.10
  7.9 0.7 copy-start.11
  76.5 1.7 %copy-start = (bf16[1,256,1536]{2,1,0:T(8,128)(2,1)S(1)}, bf16[1,256,1536]{2,1,0:T(8,128)(2,1)}, u32[]{:S(2)}) copy-start(bf16[1,256,1536]{2,1,0:T(8,128)(2,1)} %param.27) | copy-start | bytes 2359300
  76.5 1.7 %copy-start.8 = (s32[16,8]{0,1:T(8,128)S(1)}, s32[16,8]{0,1:T(8,128)}, u32[]{:S(2)}) copy-start(s32[16,8]{0,1:T(8,128)} %param.24) | copy-start | bytes 1540
  76.5 1.7 %copy-start.9 = (f32[16,8]{0,1:T(8,128)S(1)}, f32[16,8]{0,1:T(8,128)}, u32[]{:S(2)}) copy-start(f32[16,8]{0,1:T(8,128)} %param.25) | copy-start | bytes 1540

commit v3 on v2

v3 whole, which is shorter than its diff:
```python
import jax
import jax.numpy as jnp
from jax import lax
from jax.experimental import pallas as pl
from jax.experimental.pallas import tpu as pltpu
from jax.sharding import PartitionSpec as P

score_scale = 0.015625
residual_scale = 0.22
masked_score = -1e30
D_MODEL = 1536
HALF = 768
SLOTS = 32
OWN_SLOT = 12
SLAB = 8
TREE = 64
ROWS = 128
CARRIED = 160
MESH = pl.DeviceIdType.MESH


def layer_kernel(len_hbm, leaf_hbm, tok_hbm, wq_hbm, wk_hbm, wv_hbm, ck_hbm, cv_hbm, par_hbm, wo_hbm, routes_hbm, weight_hbm,
                 wgu_hbm, wdn_hbm, att_ref, mix_ref, nk_ref, nv_ref, len_ref, leaf_ref, tok_ref, wq_ref, wk_ref, wv_ref,
                 ck_ref, cv_ref, par_ref, routes_ref, weight_ref, wgu, wdn, toks, slices, wall, wout, normed_ref, made,
                 part_send, near_recv, stat_send, near_stat, far_send, far_recv, far_stat_send, far_stat, pair_send,
                 pair_recv, send, recv, half_send, half_recv, back_send, back_recv, fin_send, fin_recv, load_sem, tok_out,
                 tok_in, made_out, made_in, qa_out, qa_in, qb_out, qb_in, oa_out, oa_in, ob_out, ob_in, part_sem,
                 pair_sem, ship_out, ship_in):
    f32, bf = jnp.float32, jnp.bfloat16
    blk = lax.axis_index("blk")
    exp = lax.axis_index("expert")
    tp = lax.axis_index("tp")
    hi = lax.div(blk, 4)
    y = lax.rem(blk, 4)
    z_lo = lax.div(exp, 4)
    z = hi * 8 + z_lo
    x = lax.rem(exp, 4)
    partner = (1 - hi) * 4 + y
    z_blk, z_exp = {}, {}
    for dz in range(-4, 5):
        zz = lax.rem(z + (dz + 16), 16)
        z_blk[dz] = lax.div(zz, 8) * 4 + y
        z_exp[dz] = lax.rem(zz, 8) * 4
    x_at = {dx: lax.rem(x + dx, 4) for dx in range(4)}
    y_at = {dy: lax.rem(y + dy, 4) for dy in range(4)}

    def plane(dz, dx):
        return (z_blk[dz], z_exp[dz] + x_at[dx], tp)

    def along_z(dz):
        return plane(dz, 0)

    def along_x(dx):
        return plane(0, dx)

    def along_y(dy):
        return (hi * 4 + y_at[dy], exp, tp)

    across = (partner, exp, tp)
    sibling = (blk, exp, 1 - tp)

    def source_row(slot):
        return lax.rem(z_lo + (11 - slot), 8) * 4 + x

    def remote(src, dst, ssem, rsem, device):
        return pltpu.make_async_remote_copy(
            src_ref=src, dst_ref=dst, send_sem=ssem, recv_sem=rsem, device_id=device, device_id_type=MESH
        )

    pairs = (
        (wq_hbm, wq_ref), (wk_hbm, wk_ref), (wv_hbm, wv_ref), (tok_hbm, tok_ref), (len_hbm, len_ref),
        (leaf_hbm, leaf_ref), (par_hbm, par_ref), (routes_hbm, routes_ref), (weight_hbm, weight_ref), (ck_hbm, ck_ref),
        (cv_hbm, cv_ref), (wo_hbm, wout.at[exp]), (wgu_hbm, wgu), (wdn_hbm, wdn),
    )
    loads = [pltpu.make_async_copy(src, dst, load_sem.at[n]) for n, (src, dst) in enumerate(pairs)]
    for load in loads:
        load.start()

    barrier = pltpu.get_barrier_semaphore()

    def greet(device):
        pl.semaphore_signal(barrier, inc=1, device_id=device, device_id_type=MESH)

    for d in range(1, 8):
        greet((lax.rem(blk + d, 8), exp, tp))
    for dz in (-4, 4, -3, 3, -2, 2, -1, 1, 0):
        for dx in range(4):
            if dz or dx:
                greet(plane(dz, dx))
    greet(sibling)

    for n in range(4):
        loads[n].wait()
    for b in range(8):
        if b < 6:
            slices[b, :, 0:128] = wq_ref[:, b * 128 : (b + 1) * 128]
        else:
            slices[b, :, 0:128] = wk_ref[:, (b - 6) * 128 : (b - 5) * 128]
        slices[b, :, 128:256] = wv_ref[:, (b // 4) * 128 : (b // 4 + 1) * 128]
    wall[exp] = slices[blk]
    toks[blk] = tok_ref[...]
    pl.semaphore_wait(barrier, 43)

    def share_start(buf, ssem, rsem):
        remote(buf.at[blk], buf.at[blk], ssem.at[3], rsem.at[3], across).start()
        for d in range(1, 4):
            remote(buf.at[blk], buf.at[blk], ssem.at[d - 1], rsem.at[d - 1], along_y(d)).start()

    def share_forward(buf, ssem, rsem):
        remote(buf.at[partner], buf.at[partner], ssem.at[3], rsem.at[3], across).wait_recv()
        for d in range(1, 4):
            remote(buf.at[partner], buf.at[partner], ssem.at[3 + d], rsem.at[3 + d], along_y(d)).start()

    def share_finish(buf, ssem, rsem):
        for d in range(1, 4):
            for half in range(2):
                remote(
                    buf.at[blk], buf.at[(hi if half == 0 else 1 - hi) * 4 + y_at[4 - d]], ssem.at[d - 1 + 4 * half],
                    rsem.at[d - 1 + 4 * half], across,
                ).wait_recv()

    def share_sent(buf, ssem, rsem):
        for s in range(7):
            remote(buf.at[blk], buf.at[blk], ssem.at[s], rsem.at[s], across).wait_send()

    share_start(toks, tok_out, tok_in)

    for dz in (4, -3, 3, -2, 2, -1, 1):
        remote(slices.at[z_blk[dz]], wall.at[exp], qa_out.at[0], qa_in.at[dz + 3], along_z(dz)).start()

    def pass_on(slot, buf, ssem, rsem):
        row = source_row(slot)
        for d in range(1, 4):
            remote(buf.at[row], buf.at[row], ssem.at[0], rsem.at[0], along_x(d)).start()

    pass_on(3, wall, qb_out, qb_in)

    loads[11].wait()
    for dz in (4, -3, 3, -2, 2, -1, 1):
        remote(wout.at[exp], wout.at[exp], oa_out.at[0], oa_in.at[dz + 3], along_z(dz)).start()
    for dz in (1, -1, 2, -2, 3, -3, 4):
        row = source_row(dz + 3)
        remote(wall.at[row], wall.at[row], qa_out.at[0], qa_in.at[dz + 3], across).wait_recv()
        pass_on(dz + 3, wall, qb_out, qb_in)
    share_forward(toks, tok_out, tok_in)
    for n in range(4, 9):
        loads[n].wait()
    lane = lax.broadcasted_iota(jnp.int32, (ROWS, 128), 1)
    line = lax.broadcasted_iota(jnp.int32, (ROWS, 128), 0)
    parent = jnp.concatenate([par_ref[0:1, :], par_ref[1:2, :]], axis=1)
    parent = jnp.where(parent >= 0, parent + 64 * (lax.broadcasted_iota(jnp.int32, (1, 128), 1) // 64), -1)
    eye = jnp.where(lane == line, 1.0, 0.0)
    upward = eye + jnp.where(line == parent, 1.0, 0.0)
    for doubling in range(6):
        short = upward.astype(bf)
        upward = jnp.minimum(upward + jnp.dot(short, short, preferred_element_type=f32), 1.0)
    upward_bf = upward.astype(bf)
    dims0 = (((0,), (0,)), ((), ()))
    reach = lax.dot_general(upward_bf, eye.astype(bf), dims0, preferred_element_type=f32)
    depth = lax.dot_general(upward_bf, jnp.ones((ROWS, 128), bf), dims0, preferred_element_type=f32) - 1.0
    len0 = len_ref[0].astype(f32)
    len1 = len_ref[1].astype(f32)
    place = depth + jnp.where(line < 64, len0, len1)
    rate = jnp.exp((lane % 32).astype(f32) * (-9.210340371976184 / 32.0))
    angle = place * rate
    cos = jnp.cos(angle)
    low_half = (lane % 64) < 32
    sin = jnp.where(low_half, -1.0, 1.0) * jnp.sin(angle)
    target = jnp.sum(upward, axis=0, keepdims=True) - 1.0 + jnp.where(lane[0:1] < 64, len0, len1)
    on_path = jnp.sum(
        jnp.where((line == leaf_ref[0]) | (line == leaf_ref[1] + 64), reach, 0.0), axis=0, keepdims=True
    )

    share_finish(toks, tok_out, tok_in)

    for r in range(2):
        rows = toks[:, r].reshape(TREE, D_MODEL).astype(f32)
        scale = lax.rsqrt(jnp.mean(rows * rows, axis=-1, keepdims=True) + 1e-06)
        normed_ref[r * TREE : (r + 1) * TREE, :] = (rows * scale).astype(bf)
    remote(wall.at[pl.ds(0, 24)], wall.at[pl.ds(0, 24)], qb_out.at[0], qb_in.at[0], across).wait_recv()
    w_first = wall[:, :, 0:128].reshape(D_MODEL, 128)
    w_second = wall[:, :, 128:256].reshape(D_MODEL, 128)
    first = jnp.dot(normed_ref[...], w_first, preferred_element_type=f32)
    turned = jnp.where(low_half, pltpu.roll(first, 96, 1), pltpu.roll(first, 32, 1))
    made[blk, 0:ROWS, :] = (first * cos + turned * sin).astype(bf)
    quarter = normed_ref[pl.ds(pl.multiple_of(y * 32, 32), 32), :]
    made[blk, ROWS:CARRIED, :] = jnp.dot(quarter, w_second, preferred_element_type=f32).astype(bf)

    share_start(made, made_out, made_in)

    pass_on(3, wout, ob_out, ob_in)
    rows = 16
    mine = pl.ds(pl.multiple_of(tp * HALF, HALF), HALF)
    theirs = pl.ds(pl.multiple_of((1 - tp) * HALF, HALF), HALF)
    slot = lax.broadcasted_iota(jnp.int32, (SLOTS * SLAB, rows), 0)
    kk = slot // SLAB
    cc = slot % SLAB
    expert_of = ((z_lo + kk // 4 + 5) % 8) * 4 + (x + kk % 4) % 4
    named = jnp.zeros((SLOTS * SLAB, rows), f32)
    weighed = jnp.zeros((SLOTS * SLAB, rows), f32)
    for t in range(8):
        hit = expert_of == routes_ref[t : t + 1, :]
        named = named + jnp.where(hit, 1.0, 0.0)
        weighed = weighed + jnp.where(hit, weight_ref[t : t + 1, :], 0.0)
    earlier = jnp.where(
        lax.broadcasted_iota(jnp.int32, (rows, rows), 0) < lax.broadcasted_iota(jnp.int32, (rows, rows), 1), 1.0, 0.0
    ).astype(bf)
    rank = jnp.dot(named.astype(bf), earlier, preferred_element_type=f32)
    chosen = jnp.where((named > 0.5) & (jnp.abs(rank - cc.astype(f32)) < 0.5), 1.0, 0.0)
    weighed = weighed * chosen
    chosen_bf = chosen.astype(bf)
    w_high = weighed.astype(bf)
    w_low = (weighed - w_high.astype(f32)).astype(bf)

    share_forward(made, made_out, made_in)
    for dz in (1, -1, 2, -2, 3, -3, 4):
        row = source_row(dz + 3)
        remote(wout.at[row], wout.at[row], oa_out.at[0], oa_in.at[dz + 3], across).wait_recv()
        pass_on(dz + 3, wout, ob_out, ob_in)
    share_finish(made, made_out, made_in)

    for n in (9, 10):
        loads[n].wait()
    tree_k = [made[6 + c, 0:ROWS, :] for c in range(2)]
    tree_v = [jnp.concatenate([made[c * 4 + q, ROWS:CARRIED, :] for q in range(4)], axis=0) for c in range(2)]
    nt = (((1,), (1,)), ((), ()))
    left = lane < 64
    for r in range(2):
        length = len0 if r == 0 else len1
        sees = (lane[0:1] + blk * 128).astype(f32) < length
        tree_ok = (reach[r * TREE : (r + 1) * TREE] > 0.5) & (((lane[0:TREE] % 64) // 8) == blk)
        left64 = left[0:TREE]
        lane64 = lane[0:TREE]
        stat = jnp.zeros((TREE, 128), f32)
        tops = []
        for c in range(2):
            stack = []
            for head in range(6 * c, 6 * c + 6):
                block = made[head // 2, r * TREE : (r + 1) * TREE, :].astype(f32)
                side = (head // 3) % 2
                if side != head % 2:
                    block = pltpu.roll(block, 64, 1)
                stack.append(jnp.where(left64 if side == 0 else ~left64, block, 0.0).astype(bf))
            query = jnp.concatenate(stack, axis=0)
            cols = slice(c * 128, (c + 1) * 128)
            s_cache = lax.dot_general(query, ck_ref[r, :, cols], nt, preferred_element_type=f32) * score_scale
            s_tree = lax.dot_general(query, tree_k[c], nt, preferred_element_type=f32) * score_scale
            s_cache = jnp.where(sees, s_cache, masked_score).reshape(6, TREE, 128)
            s_tree = jnp.where(tree_ok, s_tree.reshape(6, TREE, 128), masked_score)
            peak = jnp.maximum(
                jnp.max(s_cache, axis=-1, keepdims=True), jnp.max(s_tree, axis=-1, keepdims=True)
            )
            p_cache = jnp.where(sees, jnp.exp(s_cache - peak), 0.0)
            p_tree = jnp.where(tree_ok, jnp.exp(s_tree - peak), 0.0)
            mass = jnp.sum(p_cache, axis=-1, keepdims=True) + jnp.sum(p_tree, axis=-1, keepdims=True)
            total = jnp.dot(
                p_cache.reshape(6 * TREE, 128).astype(bf), cv_ref[r, :, cols], preferred_element_type=f32
            ) + jnp.dot(p_tree.reshape(6 * TREE, 128).astype(bf), tree_v[c], preferred_element_type=f32)
            total = total.reshape(6, TREE, 128) / jnp.where(mass > 0.0, mass, 1.0)
            for n in range(6):
                head = 6 * c + n
                stat = jnp.where(lane64 == head, peak[n], stat)
                stat = jnp.where(lane64 == 64 + head, mass[n], stat)
                tops.append(total[n])
        for i in range(6):
            parts = []
            for u in range(2):
                head = 2 * i + u
                value = tops[head]
                if (head // 3) % 2 != u:
                    value = pltpu.roll(value, 64, 1)
                parts.append(value)
            joined = jnp.where(left64, parts[0], parts[1])
            part_send[:, :, r, :, i * 128 : (i + 1) * 128] = joined.astype(bf).reshape(2, 4, 8, 128)
        stat_send[:, :, r, :, :] = stat.reshape(2, 4, 8, 128)

    for group, other in ((0, 1 - hi), (1, hi)):
        for d in range(1, 4):
            remote(
                part_send.at[other, y_at[d]], near_recv.at[group, y], part_sem.at[4 * group], part_sem.at[4 * group + 1],
                along_y(d),
            ).start()
            remote(
                stat_send.at[other, y_at[d]], near_stat.at[group, y], part_sem.at[4 * group + 2],
                part_sem.at[4 * group + 3], along_y(d),
            ).start()
        near_recv[group, y] = part_send[other, y]
        near_stat[group, y] = stat_send[other, y]

    spread = jnp.where(
        lax.broadcasted_iota(jnp.int32, (128, HALF), 1) // 64 == lax.broadcasted_iota(jnp.int32, (128, HALF), 0), 1.0, 0.0
    ).astype(bf)

    def combine(count, stats, values):
        masses = pltpu.roll(stats.reshape(count * 16, 128), 64, 1).reshape(count, 16, 128)
        peak = jnp.max(stats, axis=0, keepdims=True)
        share = jnp.where(lane[0:16] < 12, masses * jnp.exp(stats - peak), 0.0)
        whole = jnp.sum(share, axis=0, keepdims=True)
        share = (share / jnp.where(whole > 0.0, whole, 1.0)).reshape(count * 16, 128)
        share_high = share.astype(bf)
        share_low = (share - share_high.astype(f32)).astype(bf)
        factor = jnp.dot(share_high, spread, preferred_element_type=f32) + jnp.dot(
            share_low, spread, preferred_element_type=f32
        )
        joined = jnp.sum(factor.reshape(count, 16, HALF) * values.reshape(count, 16, HALF).astype(f32), axis=0)
        stat = jnp.where(lane[0:16] < 12, peak[0], 0.0) + pltpu.roll(whole[0], 64, 1)
        return joined, stat

    def near_wait(group):
        for n, (out, into) in enumerate(((part_send.at[0], near_recv.at[group]), (stat_send.at[0], near_stat.at[group]))):
            remote(
                out.at[pl.ds(0, 3)], into.at[pl.ds(0, 3)], part_sem.at[4 * group + 2 * n],
                part_sem.at[4 * group + 2 * n + 1], across,
            ).wait()

    near_wait(0)
    joined, stat = combine(4, near_stat[0].reshape(4, 16, 128), near_recv[0])
    far_send[...] = joined.astype(bf)
    far_stat_send[...] = stat
    far = (
        remote(far_send, far_recv, part_sem.at[8], part_sem.at[9], across),
        remote(far_stat_send, far_stat, part_sem.at[10], part_sem.at[11], across),
    )
    for copy in far:
        copy.start()
    for r in range(2):
        spot = (line + blk * 128).astype(f32)
        placing = jnp.where((spot == target) & (on_path > 0.5) & ((lane // 64) == r), 1.0, 0.0)
        written = jnp.max(placing, axis=-1, keepdims=True) > 0.5
        placing = placing.astype(bf)
        for c in range(2):
            cols = slice(c * 128, (c + 1) * 128)
            moved_k = jnp.dot(placing, tree_k[c], preferred_element_type=f32)
            nk_ref[r, :, cols] = jnp.where(written, moved_k, ck_ref[r, :, cols].astype(f32)).astype(bf)
            moved_v = jnp.dot(placing, tree_v[c], preferred_element_type=f32)
            nv_ref[r, :, cols] = jnp.where(written, moved_v, cv_ref[r, :, cols].astype(f32)).astype(bf)
    near_wait(1)
    joined, stat = combine(4, near_stat[1].reshape(4, 16, 128), near_recv[1])
    for copy in far:
        copy.wait()
    first_peak = stat
    second_peak = far_stat[...]
    peak = jnp.maximum(first_peak, second_peak)
    pair_share = [
        jnp.where(lane[0:16] < 12, pltpu.roll(one, 64, 1) * jnp.exp(one - peak), 0.0) for one in (first_peak, second_peak)
    ]
    whole = pair_share[0] + pair_share[1]
    inverse = 1.0 / jnp.where(whole > 0.0, whole, 1.0)
    pair_share = jnp.concatenate([pair_share[0] * inverse, pair_share[1] * inverse], axis=0)
    share_high = pair_share.astype(bf)
    share_low = (pair_share - share_high.astype(f32)).astype(bf)
    factor = jnp.dot(share_high, spread, preferred_element_type=f32) + jnp.dot(
        share_low, spread, preferred_element_type=f32
    )
    context = (factor[0:16] * joined + factor[16:32] * far_recv[...].astype(f32)).astype(bf)
    remote(wout.at[pl.ds(0, 24)], wout.at[pl.ds(0, 24)], ob_out.at[0], ob_in.at[0], across).wait_recv()
    terms = lax.dot_general(context, wout[...].reshape(D_MODEL, HALF), nt, preferred_element_type=f32).astype(bf)
    pair_send[...] = terms
    pair = remote(pair_send, pair_recv, pair_sem.at[0], pair_sem.at[1], sibling)
    pair.start()
    pair.wait()
    attended = (terms.astype(f32) + pair_recv[...].astype(f32)).astype(bf)
    att_ref[...] = attended
    mixed = tok_ref[...].reshape(16, D_MODEL).astype(f32) + residual_scale * attended.astype(f32)
    scale = lax.rsqrt(jnp.mean(mixed * mixed, axis=-1, keepdims=True) + 1e-06)
    hidden_in = (mixed * scale).astype(bf)
    for own in range(2):

        @pl.when(tp == own)
        def _():
            sent = jnp.dot(chosen_bf, hidden_in[:, own * HALF : (own + 1) * HALF], preferred_element_type=f32).astype(bf)
            send[...] = sent.reshape(SLOTS, SLAB, HALF)

    recv[tp, OWN_SLOT] = send[OWN_SLOT]
    order = sorted(range(-3, 5), key=lambda d: -abs(d))
    for dz in order:
        for dx in (2, 1, 3, 0):
            k = (dz + 3) * 4 + dx
            if k != OWN_SLOT:
                remote(send.at[k], recv.at[tp, k], ship_out.at[0], ship_in.at[0], plane(dz, dx)).start()
    remote(
        send.at[pl.ds(0, 31)], recv.at[tp, pl.ds(0, 31)], ship_out.at[0], ship_in.at[0], sibling
    ).wait()
    swap = remote(recv.at[tp], recv.at[tp], pair_sem.at[2], pair_sem.at[3], sibling)
    swap.start()
    for n in (12, 13):
        loads[n].wait()
    swap.wait()
    low = recv[0].reshape(SLOTS * SLAB, HALF)
    high = recv[1].reshape(SLOTS * SLAB, HALF)

    def proj(g):
        return jnp.dot(low, wgu[g, :HALF, :], preferred_element_type=f32) + jnp.dot(
            high, wgu[g, HALF:, :], preferred_element_type=f32
        )

    gate = proj(0)
    up = proj(1)
    hidden = (gate / (1.0 + jnp.exp(-gate)) * up).astype(bf)
    half_send[...] = jnp.dot(hidden, wdn[:, theirs], preferred_element_type=f32).astype(bf)
    swap = remote(half_send, half_recv, pair_sem.at[4], pair_sem.at[5], sibling)
    swap.start()
    part = jnp.dot(hidden, wdn[:, mine], preferred_element_type=f32)
    swap.wait()
    total = (part + half_recv[...].astype(f32)).astype(bf)
    back_send[...] = total.reshape(SLOTS, SLAB, HALF)
    back_recv[OWN_SLOT] = total[OWN_SLOT * SLAB : (OWN_SLOT + 1) * SLAB]
    for dz in order:
        for dx in (2, 1, 3, 0):
            k = (dz + 3) * 4 + dx
            if k != OWN_SLOT:
                remote(
                    back_send.at[k], back_recv.at[k], ship_out.at[1], ship_in.at[1], plane(-dz, (4 - dx) % 4)
                ).start()
    remote(
        back_send.at[pl.ds(0, 31)], back_recv.at[pl.ds(0, 31)], ship_out.at[1], ship_in.at[1], sibling
    ).wait()
    got = back_recv[...].reshape(SLOTS * SLAB, HALF)
    combined = lax.dot_general(w_high, got, dims0, preferred_element_type=f32) + lax.dot_general(
        w_low, got, dims0, preferred_element_type=f32
    )
    fin_send[...] = combined.astype(bf)
    last = remote(fin_send, fin_recv, pair_sem.at[6], pair_sem.at[7], sibling)
    last.start()
    mix_ref[:, mine] = combined.astype(bf)
    last.wait()
    mix_ref[:, theirs] = fin_recv[...]

    share_sent(toks, tok_out, tok_in)
    share_sent(made, made_out, made_in)
    remote(wall.at[pl.ds(0, 7)], wall.at[pl.ds(0, 7)], qa_out.at[0], qb_in.at[0], across).wait_send()
    remote(wall.at[pl.ds(0, 24)], wall.at[pl.ds(0, 24)], qb_out.at[0], qb_in.at[0], across).wait_send()
    remote(wout.at[pl.ds(0, 7)], wout.at[pl.ds(0, 7)], oa_out.at[0], ob_in.at[0], across).wait_send()
    remote(wout.at[pl.ds(0, 24)], wout.at[pl.ds(0, 24)], ob_out.at[0], ob_in.at[0], across).wait_send()


def local(tokens, w_query, w_key, w_value, w_out, cache_keys, cache_values, parents, lengths, accepted_leaf, routes,
          route_weight, w_gateup, w_down):
    f32, bf = jnp.float32, jnp.bfloat16
    vmem = pltpu.VMEM
    keep = pl.BlockSpec(memory_space=pltpu.VMEM)
    dma = pltpu.SemaphoreType.DMA
    attended, expert_mix, new_keys, new_values = pl.pallas_call(
        layer_kernel,
        out_shape=(
            jax.ShapeDtypeStruct(tokens.shape, bf),
            jax.ShapeDtypeStruct(tokens.shape, bf),
            jax.ShapeDtypeStruct(cache_keys.shape, bf),
            jax.ShapeDtypeStruct(cache_values.shape, bf),
        ),
        in_specs=[pl.BlockSpec(memory_space=pl.ANY)] * 14,
        out_specs=(keep,) * 4,
        scratch_shapes=[
            pltpu.SMEM((2,), jnp.int32), pltpu.SMEM((2,), jnp.int32),
            vmem((2, 8, D_MODEL), bf), vmem((48, HALF), bf), vmem((48, 256), bf), vmem((48, 256), bf),
            vmem((2, 128, 256), bf), vmem((2, 128, 256), bf), vmem((2, TREE), jnp.int32), vmem((8, 16), jnp.int32),
            vmem((8, 16), f32), vmem((2, D_MODEL, 256), bf), vmem((256, D_MODEL), bf),
            vmem((8, 2, 8, D_MODEL), bf), vmem((8, 48, 256), bf), vmem((32, 48, 256), bf), vmem((32, 48, HALF), bf),
            vmem((ROWS, D_MODEL), bf), vmem((8, CARRIED, 128), bf),
            vmem((2, 4, 2, 8, HALF), bf), vmem((2, 4, 2, 8, HALF), bf), vmem((2, 4, 2, 8, 128), f32),
            vmem((2, 4, 2, 8, 128), f32), vmem((16, HALF), bf), vmem((16, HALF), bf), vmem((16, 128), f32),
            vmem((16, 128), f32), vmem((16, D_MODEL), bf), vmem((16, D_MODEL), bf),
            vmem((SLOTS, SLAB, HALF), bf), vmem((2, SLOTS, SLAB, HALF), bf), vmem((SLOTS * SLAB, HALF), bf),
            vmem((SLOTS * SLAB, HALF), bf), vmem((SLOTS, SLAB, HALF), bf), vmem((SLOTS, SLAB, HALF), bf),
            vmem((16, HALF), bf), vmem((16, HALF), bf),
            dma((14,)), dma((7,)), dma((7,)), dma((7,)), dma((7,)),
            dma((1,)), dma((8,)), dma((1,)), dma((1,)),
            dma((1,)), dma((8,)), dma((1,)), dma((1,)),
            dma((12,)), dma((8,)), dma((2,)), dma((2,)),
        ],
        compiler_params=pltpu.CompilerParams(
            collective_id=1, has_side_effects=True, vmem_limit_bytes=50 * 1024 * 1024
        ),
    )(
        lengths, accepted_leaf, tokens.reshape(2, 8, D_MODEL), w_query, w_key, w_value, cache_keys, cache_values, parents,
        w_out.T, routes.T, route_weight.T, w_gateup[0].transpose(1, 0, 2), w_down[0],
    )
    return (attended, expert_mix, new_keys, new_values)


def solution(mesh):
    in_specs = (
        P(("blk", "expert"), None),
        P("expert", "tp"),
        P("expert", "tp"),
        P("expert", "tp"),
        P("tp", "expert"),
        P("expert", "blk", "tp"),
        P("expert", "blk", "tp"),
        P("expert", None),
        P("expert"),
        P("expert"),
        P(("blk", "expert"), None),
        P(("blk", "expert"), None),
        P("expert", None, None, "tp"),
        P("expert", "tp", None),
    )
    out_specs = (
        P(("blk", "expert"), None),
        P(("blk", "expert"), None),
        P("expert", "blk", "tp"),
        P("expert", "blk", "tp"),
    )
    return jax.shard_map(local, mesh=mesh, in_specs=in_specs, out_specs=out_specs, check_vma=False)
```

time: 131 us -> 111 us (0.85)
  the two profiles are of different devices: /device:TPU:41 before, /device:TPU:1 now
where the time goes in v3:
time: 111 us
  Pallas kernels  106 us (95%)
  local copies, waits for them, and re-layouts  4.29 us (4%)
    pallas_call x1, Pallas kernels, local(): pl.pallas_call(layer_kernel, out_shape=(jax.ShapeDtypeStruct(tokens.shape...  106 us
    unnamed x31, local copies, waits for them, and re-layouts  4.29 us

profile of v3, /device:TPU:1, one launch (start us, length us, event | category | flops | bytes accessed | tf_op | source)
XLA Modules:
  0.0 110.7 jit_solution(3233802545844131096)
XLA Ops:
  0.6 0.0 copy-start
  0.6 0.0 copy-start.1
  0.7 0.0 copy-start.2
  0.7 0.0 copy-start.3
  0.7 0.0 copy-start.4
  0.7 0.0 copy-start.5
  0.7 0.0 copy-start.6
  0.7 0.0 copy-start.7
  0.7 0.0 copy-start.8
  0.7 0.0 copy-start.9
  0.7 0.0 copy-start.10
  0.7 0.0 copy-start.11
  0.8 0.0 copy-start.12
  0.8 1.7 %copy.20 = bf16[1,1536,2,256]{3,1,2,0:T(8,128)(2,1)S(1)} copy(bf16[1,1536,2,256]{3,2,1,0:T(2,128)(2,1)} %param.26) | data formatting | bytes 3145728 | tf_op args[12]
  2.5 0.0 copy-done
  2.5 0.0 copy-done.1
  2.5 0.0 copy-done.2
  2.5 0.0 copy-done.3
  2.5 0.0 copy-done.4
  2.5 0.0 copy-done.5
  2.5 0.0 copy-done.6
  2.5 0.0 copy-done.7
  2.5 0.0 copy-done.8
  2.5 0.0 copy-done.9
  2.6 0.0 copy-done.10
  2.6 0.0 copy-done.11
  2.6 0.0 copy-done.12
  2.6 105.5 %shard_map.165 = (bf16[16,1536]{1,0:T(8,128)(2,1)S(1)}, bf16[16,1536]{1,0:T(8,128)(2,1)S(1)}, bf16[2,128,256]{2,1,0:T(8,128)(2,1)S(1)}, bf16[2,128,256]{2,1,0:T(8,128)(2,1)S(1)}) custom-call(s32[2]{0:T(128)S(1)} %copy-done.11, s32[2]{0:T(128)S(1)} %copy-done.12, bf16[2,8,1536]{2,1,0:T(8,128)(2,1)S(1)} %bitcast.13, bf16[48,768]{1,0:T(8,128)(2,1)S(1)} %copy-done.3, ...), custom_call_target="tpu_custom_call" | custom-call | tf_op jit(solution)/shard_map/pallas_call | solution.py:443
  108.1 0.6 copy.25
  108.8 0.6 copy.26
  109.4 0.7 copy.27
  110.0 0.7 copy.28
Async XLA Ops:
  0.6 1.8 %copy-start = (bf16[1,256,1536]{2,1,0:T(8,128)(2,1)S(1)}, bf16[1,256,1536]{2,1,0:T(8,128)(2,1)}, u32[]{:S(2)}) copy-start(bf16[1,256,1536]{2,1,0:T(8,128)(2,1)} %param.27) | copy-start | bytes 2359300
  0.6 1.8 %copy-start.1 = (bf16[2,128,256]{2,1,0:T(8,128)(2,1)S(1)}, bf16[2,128,256]{2,1,0:T(8,128)(2,1)}, u32[]{:S(2)}) copy-start(bf16[2,128,256]{2,1,0:T(8,128)(2,1)} %ck_hbm.1) | copy-start | bytes 393220
  0.7 1.8 %copy-start.2 = (bf16[2,128,256]{2,1,0:T(8,128)(2,1)S(1)}, bf16[2,128,256]{2,1,0:T(8,128)(2,1)}, u32[]{:S(2)}) copy-start(bf16[2,128,256]{2,1,0:T(8,128)(2,1)} %cv_hbm.1) | copy-start | bytes 393220
  0.7 1.8 %copy-start.3 = (bf16[48,768]{1,0:T(8,128)(2,1)S(1)}, bf16[48,768]{1,0:T(8,128)(2,1)}, u32[]{:S(2)}) copy-start(bf16[48,768]{1,0:T(8,128)(2,1)} %wq_hbm.1) | copy-start | bytes 221188
  0.7 1.8 %copy-start.4 = (bf16[768,48]{0,1:T(8,128)(2,1)S(1)}, bf16[768,48]{0,1:T(8,128)(2,1)}, u32[]{:S(2)}) copy-start(bf16[768,48]{0,1:T(8,128)(2,1)} %param.18) | copy-start | bytes 221188
  0.7 1.8 %copy-start.5 = (bf16[16,1536]{1,0:T(8,128)(2,1)S(1)}, bf16[16,1536]{1,0:T(8,128)(2,1)}, u32[]{:S(2)}) copy-start(bf16[16,1536]{1,0:T(8,128)(2,1)} %param.14) | copy-start | bytes 147460
  0.7 1.8 %copy-start.6 = (bf16[48,256]{1,0:T(8,128)(2,1)S(1)}, bf16[48,256]{1,0:T(8,128)(2,1)}, u32[]{:S(2)}) copy-start(bf16[48,256]{1,0:T(8,128)(2,1)} %wk_hbm.1) | copy-start | bytes 73732
  0.7 1.8 %copy-start.7 = (bf16[48,256]{1,0:T(8,128)(2,1)S(1)}, bf16[48,256]{1,0:T(8,128)(2,1)}, u32[]{:S(2)}) copy-start(bf16[48,256]{1,0:T(8,128)(2,1)} %wv_hbm.1) | copy-start | bytes 73732
  0.7 1.8 %copy-start.8 = (s32[16,8]{0,1:T(8,128)S(1)}, s32[16,8]{0,1:T(8,128)}, u32[]{:S(2)}) copy-start(s32[16,8]{0,1:T(8,128)} %param.24) | copy-start | bytes 1540
  0.7 1.8 %copy-start.9 = (f32[16,8]{0,1:T(8,128)S(1)}, f32[16,8]{0,1:T(8,128)}, u32[]{:S(2)}) copy-start(f32[16,8]{0,1:T(8,128)} %param.25) | copy-start | bytes 1540
  0.7 1.8 %copy-start.10 = (s32[2,64]{1,0:T(2,128)S(1)}, s32[2,64]{1,0:T(2,128)}, u32[]{:S(2)}) copy-start(s32[2,64]{1,0:T(2,128)} %par_hbm.1) | copy-start | bytes 1540
  0.7 1.8 %copy-start.11 = (s32[2]{0:T(128)S(1)}, s32[2]{0:T(128)}, u32[]{:S(2)}) copy-start(s32[2]{0:T(128)} %len_hbm.1) | copy-start | bytes 28
  0.8 1.8 %copy-start.12 = (s32[2]{0:T(128)S(1)}, s32[2]{0:T(128)}, u32[]{:S(2)}) copy-start(s32[2]{0:T(128)} %leaf_hbm.1) | copy-start | bytes 28

commit v4 on v3

--- a/solution.py
+++ b/solution.py
@@ -16,6 +16,7 @@
 TREE = 64
 ROWS = 128
 CARRIED = 160
+PACKED = 64
 MESH = pl.DeviceIdType.MESH
 
 
@@ -24,7 +25,7 @@
                  ck_ref, cv_ref, par_ref, routes_ref, weight_ref, wgu, wdn, toks, slices, wall, wout, normed_ref, made,
                  part_send, near_recv, stat_send, near_stat, far_send, far_recv, far_stat_send, far_stat, pair_send,
                  pair_recv, send, recv, half_send, half_recv, back_send, back_recv, fin_send, fin_recv, load_sem, tok_out,
-                 tok_in, made_out, made_in, qa_out, qa_in, qb_out, qb_in, oa_out, oa_in, ob_out, ob_in, part_sem,
+                 tok_in, made_out, made_in, qa_out, qa_in, qb_out, qb_in, oa_out, oa_in, ob_out, ob_in, oy_out, oy_in, part_sem,
                  pair_sem, ship_out, ship_in):
     f32, bf = jnp.float32, jnp.bfloat16
     blk = lax.axis_index("blk")
@@ -73,8 +74,13 @@
         (cv_hbm, cv_ref), (wo_hbm, wout.at[exp]), (wgu_hbm, wgu), (wdn_hbm, wdn),
     )
     loads = [pltpu.make_async_copy(src, dst, load_sem.at[n]) for n, (src, dst) in enumerate(pairs)]
-    for load in loads:
-        load.start()
+    parity = lax.rem(y, 2)
+    gives = lax.rem(z_lo + y, 2) == 0
+    for n, load in enumerate(loads):
+        if n == 11:
+            pl.when(gives)(load.start)
+        else:
+            load.start()
 
     barrier = pltpu.get_barrier_semaphore()
 
@@ -91,12 +97,19 @@
 
     for n in range(4):
         loads[n].wait()
+    group16 = lax.broadcasted_iota(jnp.int32, (16, 128), 1) // 32
     for b in range(8):
         if b < 6:
-            slices[b, :, 0:128] = wq_ref[:, b * 128 : (b + 1) * 128]
+            slices[b, 0:48, :] = wq_ref[:, b * 128 : (b + 1) * 128]
         else:
-            slices[b, :, 0:128] = wk_ref[:, (b - 6) * 128 : (b - 5) * 128]
-        slices[b, :, 128:256] = wv_ref[:, (b // 4) * 128 : (b // 4 + 1) * 128]
+            slices[b, 0:48, :] = wk_ref[:, (b - 6) * 128 : (b - 5) * 128]
+        fold = jnp.zeros((16, 128), f32)
+        for g in range(3):
+            piece = wv_ref[16 * g : 16 * g + 16, (b // 4) * 128 : (b // 4 + 1) * 128].astype(f32)
+            turn = (32 * (g - b % 4)) % 128
+            piece = pltpu.roll(piece, turn, 1) if turn else piece
+            fold = jnp.where(group16 == g, piece, fold)
+        slices[b, 48:PACKED, :] = fold.astype(bf)
     wall[exp] = slices[blk]
     toks[blk] = tok_ref[...]
     pl.semaphore_wait(barrier, 43)
@@ -135,9 +148,12 @@
 
     pass_on(3, wall, qb_out, qb_in)
 
-    loads[11].wait()
-    for dz in (4, -3, 3, -2, 2, -1, 1):
-        remote(wout.at[exp], wout.at[exp], oa_out.at[0], oa_in.at[dz + 3], along_z(dz)).start()
+    @pl.when(gives)
+    def _():
+        loads[11].wait()
+        for dz in (4, -3, 3, -2, 2, -1, 1):
+            remote(wout.at[exp], wout.at[exp], oa_out.at[0], oa_in.at[dz + 3], along_z(dz)).start()
+
     for dz in (1, -1, 2, -2, 3, -3, 4):
         row = source_row(dz + 3)
         remote(wall.at[row], wall.at[row], qa_out.at[0], qa_in.at[dz + 3], across).wait_recv()
@@ -178,17 +194,41 @@
         scale = lax.rsqrt(jnp.mean(rows * rows, axis=-1, keepdims=True) + 1e-06)
         normed_ref[r * TREE : (r + 1) * TREE, :] = (rows * scale).astype(bf)
     remote(wall.at[pl.ds(0, 24)], wall.at[pl.ds(0, 24)], qb_out.at[0], qb_in.at[0], across).wait_recv()
-    w_first = wall[:, :, 0:128].reshape(D_MODEL, 128)
-    w_second = wall[:, :, 128:256].reshape(D_MODEL, 128)
+    w_first = wall[:, 0:48, :].reshape(D_MODEL, 128)
+    folded = wall[:, 48:PACKED, :].astype(f32)
+    group = lax.broadcasted_iota(jnp.int32, (32, 16, 128), 2) // 32
+    w_second = jnp.concatenate([jnp.where(group == g, folded, 0.0) for g in range(3)], axis=1)
+    w_second = w_second.astype(bf).reshape(D_MODEL, 128)
     first = jnp.dot(normed_ref[...], w_first, preferred_element_type=f32)
     turned = jnp.where(low_half, pltpu.roll(first, 96, 1), pltpu.roll(first, 32, 1))
     made[blk, 0:ROWS, :] = (first * cos + turned * sin).astype(bf)
-    quarter = normed_ref[pl.ds(pl.multiple_of(y * 32, 32), 32), :]
-    made[blk, ROWS:CARRIED, :] = jnp.dot(quarter, w_second, preferred_element_type=f32).astype(bf)
+    second = jnp.dot(normed_ref[...], w_second, preferred_element_type=f32)
+    second = second + pltpu.roll(second, 96, 1) + pltpu.roll(second, 64, 1)
+    line_group = lane[0:32] // 32
+    carried = jnp.zeros((32, 128), f32)
+    for q in range(4):
+        piece = second[32 * q : 32 * q + 32]
+        piece = pltpu.roll(piece, 32 * q, 1) if q else piece
+        carried = jnp.where(line_group == q, piece, carried)
+    made[blk, ROWS:CARRIED, :] = carried.astype(bf)
 
     share_start(made, made_out, made_in)
 
-    pass_on(3, wout, ob_out, ob_in)
+    for dz in (0, 1, -1, 2, -2, 3, -3, 4):
+        row = source_row(dz + 3)
+        source_z = lax.rem(z_lo + (8 - dz), 8)
+
+        @pl.when(lax.rem(source_z + parity, 2) == 0)
+        def _(dz=dz, row=row, source_z=source_z):
+            if dz:
+                remote(wout.at[row], wout.at[row], oa_out.at[0], oa_in.at[dz + 3], across).wait_recv()
+            for d in range(1, 4):
+                remote(
+                    wout.at[row], wout.at[row], ob_out.at[0], ob_in.at[lax.div(source_z, 2)], along_x(d)
+                ).start()
+            near_y = (hi * 4 + lax.rem(y + 1 + 2 * lax.div(source_z, 4), 4), exp, tp)
+            remote(wout.at[row], wout.at[row], oy_out.at[0], oy_in.at[0], near_y).start()
+
     rows = 16
     mine = pl.ds(pl.multiple_of(tp * HALF, HALF), HALF)
     theirs = pl.ds(pl.multiple_of((1 - tp) * HALF, HALF), HALF)
@@ -213,16 +253,23 @@
     w_low = (weighed - w_high.astype(f32)).astype(bf)
 
     share_forward(made, made_out, made_in)
-    for dz in (1, -1, 2, -2, 3, -3, 4):
-        row = source_row(dz + 3)
-        remote(wout.at[row], wout.at[row], oa_out.at[0], oa_in.at[dz + 3], across).wait_recv()
-        pass_on(dz + 3, wout, ob_out, ob_in)
     share_finish(made, made_out, made_in)
 
     for n in (9, 10):
         loads[n].wait()
     tree_k = [made[6 + c, 0:ROWS, :] for c in range(2)]
-    tree_v = [jnp.concatenate([made[c * 4 + q, ROWS:CARRIED, :] for q in range(4)], axis=0) for c in range(2)]
+    tree_v = []
+    for c in range(2):
+        quarters = []
+        for q in range(4):
+            whole = jnp.zeros((32, 128), f32)
+            for g in range(4):
+                piece = made[4 * c + g, ROWS:CARRIED, :].astype(f32)
+                turn = (32 * (g - q)) % 128
+                piece = pltpu.roll(piece, turn, 1) if turn else piece
+                whole = jnp.where(line_group == g, piece, whole)
+            quarters.append(whole)
+        tree_v.append(jnp.concatenate(quarters, axis=0).astype(bf))
     nt = (((1,), (1,)), ((), ()))
     left = lane < 64
     for r in range(2):
@@ -313,6 +360,11 @@
                 part_sem.at[4 * group + 2 * n + 1], across,
             ).wait()
 
+    for g in range(4):
+        remote(wout.at[pl.ds(0, 3)], wout.at[pl.ds(0, 3)], ob_out.at[0], ob_in.at[g], across).wait_recv()
+        for d in range(1, 4):
+            row = (2 * g + parity) * 4 + x_at[d]
+            remote(wout.at[row], wout.at[row], oy_out.at[0], oy_in.at[0], along_y(1 if g < 2 else 3)).start()
     near_wait(0)
     joined, stat = combine(4, near_stat[0].reshape(4, 16, 128), near_recv[0])
     far_send[...] = joined.astype(bf)
@@ -353,7 +405,7 @@
         share_low, spread, preferred_element_type=f32
     )
     context = (factor[0:16] * joined + factor[16:32] * far_recv[...].astype(f32)).astype(bf)
-    remote(wout.at[pl.ds(0, 24)], wout.at[pl.ds(0, 24)], ob_out.at[0], ob_in.at[0], across).wait_recv()
+    remote(wout.at[pl.ds(0, 16)], wout.at[pl.ds(0, 16)], oy_out.at[0], oy_in.at[0], across).wait()
     terms = lax.dot_general(context, wout[...].reshape(D_MODEL, HALF), nt, preferred_element_type=f32).astype(bf)
     pair_send[...] = terms
     pair = remote(pair_send, pair_recv, pair_sem.at[0], pair_sem.at[1], sibling)
@@ -430,8 +482,12 @@
     share_sent(made, made_out, made_in)
     remote(wall.at[pl.ds(0, 7)], wall.at[pl.ds(0, 7)], qa_out.at[0], qb_in.at[0], across).wait_send()
     remote(wall.at[pl.ds(0, 24)], wall.at[pl.ds(0, 24)], qb_out.at[0], qb_in.at[0], across).wait_send()
-    remote(wout.at[pl.ds(0, 7)], wout.at[pl.ds(0, 7)], oa_out.at[0], ob_in.at[0], across).wait_send()
-    remote(wout.at[pl.ds(0, 24)], wout.at[pl.ds(0, 24)], ob_out.at[0], ob_in.at[0], across).wait_send()
+
+    @pl.when(gives)
+    def _():
+        remote(wout.at[pl.ds(0, 7)], wout.at[pl.ds(0, 7)], oa_out.at[0], ob_in.at[0], across).wait_send()
+
+    remote(wout.at[pl.ds(0, 12)], wout.at[pl.ds(0, 12)], ob_out.at[0], ob_in.at[0], across).wait_send()
 
 
 def local(tokens, w_query, w_key, w_value, w_out, cache_keys, cache_values, parents, lengths, accepted_leaf, routes,
@@ -455,7 +511,7 @@
             vmem((2, 8, D_MODEL), bf), vmem((48, HALF), bf), vmem((48, 256), bf), vmem((48, 256), bf),
             vmem((2, 128, 256), bf), vmem((2, 128, 256), bf), vmem((2, TREE), jnp.int32), vmem((8, 16), jnp.int32),
             vmem((8, 16), f32), vmem((2, D_MODEL, 256), bf), vmem((256, D_MODEL), bf),
-            vmem((8, 2, 8, D_MODEL), bf), vmem((8, 48, 256), bf), vmem((32, 48, 256), bf), vmem((32, 48, HALF), bf),
+            vmem((8, 2, 8, D_MODEL), bf), vmem((8, PACKED, 128), bf), vmem((32, PACKED, 128), bf), vmem((32, 48, HALF), bf),
             vmem((ROWS, D_MODEL), bf), vmem((8, CARRIED, 128), bf),
             vmem((2, 4, 2, 8, HALF), bf), vmem((2, 4, 2, 8, HALF), bf), vmem((2, 4, 2, 8, 128), f32),
             vmem((2, 4, 2, 8, 128), f32), vmem((16, HALF), bf), vmem((16, HALF), bf), vmem((16, 128), f32),
@@ -465,7 +521,7 @@
             vmem((16, HALF), bf), vmem((16, HALF), bf),
             dma((14,)), dma((7,)), dma((7,)), dma((7,)), dma((7,)),
             dma((1,)), dma((8,)), dma((1,)), dma((1,)),
-            dma((1,)), dma((8,)), dma((1,)), dma((1,)),
+            dma((1,)), dma((8,)), dma((1,)), dma((4,)), dma((1,)), dma((1,)),
             dma((12,)), dma((8,)), dma((2,)), dma((2,)),
         ],
         compiler_params=pltpu.CompilerParams(

time: 111 us -> 104 us (0.937)
  Pallas kernels: 106 us -> 98.6 us
    pallas_call x1, Pallas kernels: 106 us -> 98.6 us  [local(): pl.pallas_call(layer_kernel, out_shape=(jax.ShapeDtypeStruct(tokens.shape...]
where the time goes in v4:
time: 104 us
  Pallas kernels  98.6 us (95%)
  local copies, waits for them, and re-layouts  4.29 us (4%)
    pallas_call x1, Pallas kernels, local(): pl.pallas_call(layer_kernel, out_shape=(jax.ShapeDtypeStruct(tokens.shape...  98.6 us
    unnamed x31, local copies, waits for them, and re-layouts  4.29 us

profile of v4, /device:TPU:1, one launch (start us, length us, event | category | flops | bytes accessed | tf_op | source)
XLA Modules:
  0.0 103.7 jit_solution(11703208038630370885)
XLA Ops:
  0.6 0.0 copy-start
  0.6 0.0 copy-start.1
  0.7 0.0 copy-start.2
  0.7 0.0 copy-start.3
  0.7 0.0 copy-start.4
  0.7 0.0 copy-start.5
  0.7 0.0 copy-start.6
  0.7 0.0 copy-start.7
  0.7 0.0 copy-start.8
  0.7 0.0 copy-start.9
  0.7 0.0 copy-start.10
  0.7 0.0 copy-start.11
  0.8 0.0 copy-start.12
  0.8 1.7 %copy.20 = bf16[1,1536,2,256]{3,1,2,0:T(8,128)(2,1)S(1)} copy(bf16[1,1536,2,256]{3,2,1,0:T(2,128)(2,1)} %param.26) | data formatting | bytes 3145728 | tf_op args[12]
  2.5 0.0 copy-done
  2.5 0.0 copy-done.1
  2.5 0.0 copy-done.2
  2.5 0.0 copy-done.3
  2.5 0.0 copy-done.4
  2.5 0.0 copy-done.5
  2.5 0.0 copy-done.6
  2.5 0.0 copy-done.7
  2.5 0.0 copy-done.8
  2.5 0.0 copy-done.9
  2.6 0.0 copy-done.10
  2.6 0.0 copy-done.11
  2.6 0.0 copy-done.12
  2.6 98.6 %shard_map.165 = (bf16[16,1536]{1,0:T(8,128)(2,1)S(1)}, bf16[16,1536]{1,0:T(8,128)(2,1)S(1)}, bf16[2,128,256]{2,1,0:T(8,128)(2,1)S(1)}, bf16[2,128,256]{2,1,0:T(8,128)(2,1)S(1)}) custom-call(s32[2]{0:T(128)S(1)} %copy-done.11, s32[2]{0:T(128)S(1)} %copy-done.12, bf16[2,8,1536]{2,1,0:T(8,128)(2,1)S(1)} %bitcast.13, bf16[48,768]{1,0:T(8,128)(2,1)S(1)} %copy-done.3, ...), custom_call_target="tpu_custom_call" | custom-call | tf_op jit(solution)/shard_map/pallas_call | solution.py:499
  101.2 0.6 copy.25
  101.8 0.6 copy.26
  102.4 0.7 copy.27
  103.1 0.7 copy.28
Async XLA Ops:
  0.6 1.8 %copy-start = (bf16[1,256,1536]{2,1,0:T(8,128)(2,1)S(1)}, bf16[1,256,1536]{2,1,0:T(8,128)(2,1)}, u32[]{:S(2)}) copy-start(bf16[1,256,1536]{2,1,0:T(8,128)(2,1)} %param.27) | copy-start | bytes 2359300
  0.6 1.8 %copy-start.1 = (bf16[2,128,256]{2,1,0:T(8,128)(2,1)S(1)}, bf16[2,128,256]{2,1,0:T(8,128)(2,1)}, u32[]{:S(2)}) copy-start(bf16[2,128,256]{2,1,0:T(8,128)(2,1)} %ck_hbm.1) | copy-start | bytes 393220
  0.7 1.8 %copy-start.2 = (bf16[2,128,256]{2,1,0:T(8,128)(2,1)S(1)}, bf16[2,128,256]{2,1,0:T(8,128)(2,1)}, u32[]{:S(2)}) copy-start(bf16[2,128,256]{2,1,0:T(8,128)(2,1)} %cv_hbm.1) | copy-start | bytes 393220
  0.7 1.8 %copy-start.3 = (bf16[48,768]{1,0:T(8,128)(2,1)S(1)}, bf16[48,768]{1,0:T(8,128)(2,1)}, u32[]{:S(2)}) copy-start(bf16[48,768]{1,0:T(8,128)(2,1)} %wq_hbm.1) | copy-start | bytes 221188
  0.7 1.8 %copy-start.4 = (bf16[768,48]{0,1:T(8,128)(2,1)S(1)}, bf16[768,48]{0,1:T(8,128)(2,1)}, u32[]{:S(2)}) copy-start(bf16[768,48]{0,1:T(8,128)(2,1)} %param.18) | copy-start | bytes 221188
  0.7 1.8 %copy-start.5 = (bf16[16,1536]{1,0:T(8,128)(2,1)S(1)}, bf16[16,1536]{1,0:T(8,128)(2,1)}, u32[]{:S(2)}) copy-start(bf16[16,1536]{1,0:T(8,128)(2,1)} %param.14) | copy-start | bytes 147460
  0.7 1.8 %copy-start.6 = (bf16[48,256]{1,0:T(8,128)(2,1)S(1)}, bf16[48,256]{1,0:T(8,128)(2,1)}, u32[]{:S(2)}) copy-start(bf16[48,256]{1,0:T(8,128)(2,1)} %wk_hbm.1) | copy-start | bytes 73732
  0.7 1.8 %copy-start.7 = (bf16[48,256]{1,0:T(8,128)(2,1)S(1)}, bf16[48,256]{1,0:T(8,128)(2,1)}, u32[]{:S(2)}) copy-start(bf16[48,256]{1,0:T(8,128)(2,1)} %wv_hbm.1) | copy-start | bytes 73732
  0.7 1.8 %copy-start.8 = (s32[16,8]{0,1:T(8,128)S(1)}, s32[16,8]{0,1:T(8,128)}, u32[]{:S(2)}) copy-start(s32[16,8]{0,1:T(8,128)} %param.24) | copy-start | bytes 1540
  0.7 1.8 %copy-start.9 = (f32[16,8]{0,1:T(8,128)S(1)}, f32[16,8]{0,1:T(8,128)}, u32[]{:S(2)}) copy-start(f32[16,8]{0,1:T(8,128)} %param.25) | copy-start | bytes 1540
  0.7 1.8 %copy-start.10 = (s32[2,64]{1,0:T(2,128)S(1)}, s32[2,64]{1,0:T(2,128)}, u32[]{:S(2)}) copy-start(s32[2,64]{1,0:T(2,128)} %par_hbm.1) | copy-start | bytes 1540
  0.7 1.8 %copy-start.11 = (s32[2]{0:T(128)S(1)}, s32[2]{0:T(128)}, u32[]{:S(2)}) copy-start(s32[2]{0:T(128)} %len_hbm.1) | copy-start | bytes 28
  0.8 1.8 %copy-start.12 = (s32[2]{0:T(128)S(1)}, s32[2]{0:T(128)}, u32[]{:S(2)}) copy-start(s32[2]{0:T(128)} %leaf_hbm.1) | copy-start | bytes 28

commit v5 on v4

--- a/solution.py
+++ b/solution.py
@@ -79,7 +79,7 @@
     for n, load in enumerate(loads):
         if n == 11:
             pl.when(gives)(load.start)
-        else:
+        elif n < 9:
             load.start()
 
     barrier = pltpu.get_barrier_semaphore()
@@ -136,8 +136,6 @@
         for s in range(7):
             remote(buf.at[blk], buf.at[blk], ssem.at[s], rsem.at[s], across).wait_send()
 
-    share_start(toks, tok_out, tok_in)
-
     for dz in (4, -3, 3, -2, 2, -1, 1):
         remote(slices.at[z_blk[dz]], wall.at[exp], qa_out.at[0], qa_in.at[dz + 3], along_z(dz)).start()
 
@@ -146,7 +144,10 @@
         for d in range(1, 4):
             remote(buf.at[row], buf.at[row], ssem.at[0], rsem.at[0], along_x(d)).start()
 
+    share_start(toks, tok_out, tok_in)
     pass_on(3, wall, qb_out, qb_in)
+    for n in (9, 10, 12, 13):
+        loads[n].start()
 
     @pl.when(gives)
     def _():
@@ -187,6 +188,29 @@
         jnp.where((line == leaf_ref[0]) | (line == leaf_ref[1] + 64), reach, 0.0), axis=0, keepdims=True
     )
 
+    rows = 16
+    mine = pl.ds(pl.multiple_of(tp * HALF, HALF), HALF)
+    theirs = pl.ds(pl.multiple_of((1 - tp) * HALF, HALF), HALF)
+    slot = lax.broadcasted_iota(jnp.int32, (SLOTS * SLAB, rows), 0)
+    kk = slot // SLAB
+    cc = slot % SLAB
+    expert_of = ((z_lo + kk // 4 + 5) % 8) * 4 + (x + kk % 4) % 4
+    named = jnp.zeros((SLOTS * SLAB, rows), f32)
+    weighed = jnp.zeros((SLOTS * SLAB, rows), f32)
+    for t in range(8):
+        hit = expert_of == routes_ref[t : t + 1, :]
+        named = named + jnp.where(hit, 1.0, 0.0)
+        weighed = weighed + jnp.where(hit, weight_ref[t : t + 1, :], 0.0)
+    earlier = jnp.where(
+        lax.broadcasted_iota(jnp.int32, (rows, rows), 0) < lax.broadcasted_iota(jnp.int32, (rows, rows), 1), 1.0, 0.0
+    ).astype(bf)
+    rank = jnp.dot(named.astype(bf), earlier, preferred_element_type=f32)
+    chosen = jnp.where((named > 0.5) & (jnp.abs(rank - cc.astype(f32)) < 0.5), 1.0, 0.0)
+    weighed = weighed * chosen
+    chosen_bf = chosen.astype(bf)
+    w_high = weighed.astype(bf)
+    w_low = (weighed - w_high.astype(f32)).astype(bf)
+
     share_finish(toks, tok_out, tok_in)
 
     for r in range(2):
@@ -228,29 +252,6 @@
                 ).start()
             near_y = (hi * 4 + lax.rem(y + 1 + 2 * lax.div(source_z, 4), 4), exp, tp)
             remote(wout.at[row], wout.at[row], oy_out.at[0], oy_in.at[0], near_y).start()
-
-    rows = 16
-    mine = pl.ds(pl.multiple_of(tp * HALF, HALF), HALF)
-    theirs = pl.ds(pl.multiple_of((1 - tp) * HALF, HALF), HALF)
-    slot = lax.broadcasted_iota(jnp.int32, (SLOTS * SLAB, rows), 0)
-    kk = slot // SLAB
-    cc = slot % SLAB
-    expert_of = ((z_lo + kk // 4 + 5) % 8) * 4 + (x + kk % 4) % 4
-    named = jnp.zeros((SLOTS * SLAB, rows), f32)
-    weighed = jnp.zeros((SLOTS * SLAB, rows), f32)
-    for t in range(8):
-        hit = expert_of == routes_ref[t : t + 1, :]
-        named = named + jnp.where(hit, 1.0, 0.0)
-        weighed = weighed + jnp.where(hit, weight_ref[t : t + 1, :], 0.0)
-    earlier = jnp.where(
-        lax.broadcasted_iota(jnp.int32, (rows, rows), 0) < lax.broadcasted_iota(jnp.int32, (rows, rows), 1), 1.0, 0.0
-    ).astype(bf)
-    rank = jnp.dot(named.astype(bf), earlier, preferred_element_type=f32)
-    chosen = jnp.where((named > 0.5) & (jnp.abs(rank - cc.astype(f32)) < 0.5), 1.0, 0.0)
-    weighed = weighed * chosen
-    chosen_bf = chosen.astype(bf)
-    w_high = weighed.astype(bf)
-    w_low = (weighed - w_high.astype(f32)).astype(bf)
 
     share_forward(made, made_out, made_in)
     share_finish(made, made_out, made_in)
@@ -375,17 +376,6 @@
     )
     for copy in far:
         copy.start()
-    for r in range(2):
-        spot = (line + blk * 128).astype(f32)
-        placing = jnp.where((spot == target) & (on_path > 0.5) & ((lane // 64) == r), 1.0, 0.0)
-        written = jnp.max(placing, axis=-1, keepdims=True) > 0.5
-        placing = placing.astype(bf)
-        for c in range(2):
-            cols = slice(c * 128, (c + 1) * 128)
-            moved_k = jnp.dot(placing, tree_k[c], preferred_element_type=f32)
-            nk_ref[r, :, cols] = jnp.where(written, moved_k, ck_ref[r, :, cols].astype(f32)).astype(bf)
-            moved_v = jnp.dot(placing, tree_v[c], preferred_element_type=f32)
-            nv_ref[r, :, cols] = jnp.where(written, moved_v, cv_ref[r, :, cols].astype(f32)).astype(bf)
     near_wait(1)
     joined, stat = combine(4, near_stat[1].reshape(4, 16, 128), near_recv[1])
     for copy in far:
@@ -430,6 +420,18 @@
             k = (dz + 3) * 4 + dx
             if k != OWN_SLOT:
                 remote(send.at[k], recv.at[tp, k], ship_out.at[0], ship_in.at[0], plane(dz, dx)).start()
+    for r in range(2):
+        spot = (line + blk * 128).astype(f32)
+        placing = jnp.where((spot == target) & (on_path > 0.5) & ((lane // 64) == r), 1.0, 0.0)
+        written = jnp.max(placing, axis=-1, keepdims=True) > 0.5
+        placing = placing.astype(bf)
+        for c in range(2):
+            cols = slice(c * 128, (c + 1) * 128)
+            moved_k = jnp.dot(placing, tree_k[c], preferred_element_type=f32)
+            nk_ref[r, :, cols] = jnp.where(written, moved_k, ck_ref[r, :, cols].astype(f32)).astype(bf)
+            moved_v = jnp.dot(placing, tree_v[c], preferred_element_type=f32)
+            nv_ref[r, :, cols] = jnp.where(written, moved_v, cv_ref[r, :, cols].astype(f32)).astype(bf)
+
     remote(
         send.at[pl.ds(0, 31)], recv.at[tp, pl.ds(0, 31)], ship_out.at[0], ship_in.at[0], sibling
     ).wait()
@@ -449,21 +451,29 @@
     gate = proj(0)
     up = proj(1)
     hidden = (gate / (1.0 + jnp.exp(-gate)) * up).astype(bf)
-    half_send[...] = jnp.dot(hidden, wdn[:, theirs], preferred_element_type=f32).astype(bf)
-    swap = remote(half_send, half_recv, pair_sem.at[4], pair_sem.at[5], sibling)
-    swap.start()
+    swaps = []
+    half_rows = SLOTS * SLAB // 2
+    for h in (1, 0):
+        span = slice(h * half_rows, (h + 1) * half_rows)
+        half_send[span, :] = jnp.dot(hidden[span], wdn[:, theirs], preferred_element_type=f32).astype(bf)
+        swap = remote(half_send.at[span], half_recv.at[span], pair_sem.at[4 + 4 * h], pair_sem.at[5 + 4 * h], sibling)
+        swap.start()
+        swaps.append(swap)
     part = jnp.dot(hidden, wdn[:, mine], preferred_element_type=f32)
-    swap.wait()
-    total = (part + half_recv[...].astype(f32)).astype(bf)
-    back_send[...] = total.reshape(SLOTS, SLAB, HALF)
-    back_recv[OWN_SLOT] = total[OWN_SLOT * SLAB : (OWN_SLOT + 1) * SLAB]
-    for dz in order:
-        for dx in (2, 1, 3, 0):
-            k = (dz + 3) * 4 + dx
-            if k != OWN_SLOT:
-                remote(
-                    back_send.at[k], back_recv.at[k], ship_out.at[1], ship_in.at[1], plane(-dz, (4 - dx) % 4)
-                ).start()
+    for h, swap in zip((1, 0), swaps):
+        span = slice(h * half_rows, (h + 1) * half_rows)
+        swap.wait()
+        total = (part[span] + half_recv[span, :].astype(f32)).astype(bf)
+        back_send[h * 16 : h * 16 + 16] = total.reshape(16, SLAB, HALF)
+        if h == 0:
+            back_recv[OWN_SLOT] = total[OWN_SLOT * SLAB : (OWN_SLOT + 1) * SLAB]
+        for dz in [d for d in order if (d + 3) // 4 == h]:
+            for dx in (2, 1, 3, 0):
+                k = (dz + 3) * 4 + dx
+                if k != OWN_SLOT:
+                    remote(
+                        back_send.at[k], back_recv.at[k], ship_out.at[1], ship_in.at[1], plane(-dz, (4 - dx) % 4)
+                    ).start()
     remote(
         back_send.at[pl.ds(0, 31)], back_recv.at[pl.ds(0, 31)], ship_out.at[1], ship_in.at[1], sibling
     ).wait()
@@ -522,7 +532,7 @@
             dma((14,)), dma((7,)), dma((7,)), dma((7,)), dma((7,)),
             dma((1,)), dma((8,)), dma((1,)), dma((1,)),
             dma((1,)), dma((8,)), dma((1,)), dma((4,)), dma((1,)), dma((1,)),
-            dma((12,)), dma((8,)), dma((2,)), dma((2,)),
+            dma((12,)), dma((10,)), dma((2,)), dma((2,)),
         ],
         compiler_params=pltpu.CompilerParams(
             collective_id=1, has_side_effects=True, vmem_limit_bytes=50 * 1024 * 1024

time: 104 us -> 103 us (level)
  Pallas kernels: 98.6 us -> 97.4 us
    pallas_call x1, Pallas kernels: 98.6 us -> 97.4 us  [local(): pl.pallas_call(layer_kernel, out_shape=(jax.ShapeDtypeStruct(tokens.shape...]
where the time goes in v5:
time: 103 us
  Pallas kernels  97.4 us (95%)
  local copies, waits for them, and re-layouts  4.29 us (4%)
    pallas_call x1, Pallas kernels, local(): pl.pallas_call(layer_kernel, out_shape=(jax.ShapeDtypeStruct(tokens.shape...  97.4 us
    unnamed x31, local copies, waits for them, and re-layouts  4.29 us

profile of v5, /device:TPU:1, one launch (start us, length us, event | category | flops | bytes accessed | tf_op | source)
XLA Modules:
  0.0 102.6 jit_solution(6423542707013067525)
XLA Ops:
  0.6 0.0 copy-start
  0.6 0.0 copy-start.1
  0.7 0.0 copy-start.2
  0.7 0.0 copy-start.3
  0.7 0.0 copy-start.4
  0.7 0.0 copy-start.5
  0.7 0.0 copy-start.6
  0.7 0.0 copy-start.7
  0.7 0.0 copy-start.8
  0.7 0.0 copy-start.9
  0.7 0.0 copy-start.10
  0.7 0.0 copy-start.11
  0.8 0.0 copy-start.12
  0.8 1.7 %copy.20 = bf16[1,1536,2,256]{3,1,2,0:T(8,128)(2,1)S(1)} copy(bf16[1,1536,2,256]{3,2,1,0:T(2,128)(2,1)} %param.26) | data formatting | bytes 3145728 | tf_op args[12]
  2.5 0.0 copy-done
  2.5 0.0 copy-done.1
  2.5 0.0 copy-done.2
  2.5 0.0 copy-done.3
  2.5 0.0 copy-done.4
  2.5 0.0 copy-done.5
  2.5 0.0 copy-done.6
  2.5 0.0 copy-done.7
  2.5 0.0 copy-done.8
  2.5 0.0 copy-done.9
  2.6 0.0 copy-done.10
  2.6 0.0 copy-done.11
  2.6 0.0 copy-done.12
  2.6 97.4 %shard_map.165 = (bf16[16,1536]{1,0:T(8,128)(2,1)S(1)}, bf16[16,1536]{1,0:T(8,128)(2,1)S(1)}, bf16[2,128,256]{2,1,0:T(8,128)(2,1)S(1)}, bf16[2,128,256]{2,1,0:T(8,128)(2,1)S(1)}) custom-call(s32[2]{0:T(128)S(1)} %copy-done.11, s32[2]{0:T(128)S(1)} %copy-done.12, bf16[2,8,1536]{2,1,0:T(8,128)(2,1)S(1)} %bitcast.13, bf16[48,768]{1,0:T(8,128)(2,1)S(1)} %copy-done.3, ...), custom_call_target="tpu_custom_call" | custom-call | tf_op jit(solution)/shard_map/pallas_call | solution.py:509
  100.0 0.6 copy.25
  100.6 0.6 copy.26
  101.3 0.7 copy.27
  101.9 0.7 copy.28
Async XLA Ops:
  0.6 1.8 %copy-start = (bf16[1,256,1536]{2,1,0:T(8,128)(2,1)S(1)}, bf16[1,256,1536]{2,1,0:T(8,128)(2,1)}, u32[]{:S(2)}) copy-start(bf16[1,256,1536]{2,1,0:T(8,128)(2,1)} %param.27) | copy-start | bytes 2359300
  0.6 1.8 %copy-start.1 = (bf16[2,128,256]{2,1,0:T(8,128)(2,1)S(1)}, bf16[2,128,256]{2,1,0:T(8,128)(2,1)}, u32[]{:S(2)}) copy-start(bf16[2,128,256]{2,1,0:T(8,128)(2,1)} %ck_hbm.1) | copy-start | bytes 393220
  0.7 1.8 %copy-start.2 = (bf16[2,128,256]{2,1,0:T(8,128)(2,1)S(1)}, bf16[2,128,256]{2,1,0:T(8,128)(2,1)}, u32[]{:S(2)}) copy-start(bf16[2,128,256]{2,1,0:T(8,128)(2,1)} %cv_hbm.1) | copy-start | bytes 393220
  0.7 1.8 %copy-start.3 = (bf16[48,768]{1,0:T(8,128)(2,1)S(1)}, bf16[48,768]{1,0:T(8,128)(2,1)}, u32[]{:S(2)}) copy-start(bf16[48,768]{1,0:T(8,128)(2,1)} %wq_hbm.1) | copy-start | bytes 221188
  0.7 1.8 %copy-start.4 = (bf16[768,48]{0,1:T(8,128)(2,1)S(1)}, bf16[768,48]{0,1:T(8,128)(2,1)}, u32[]{:S(2)}) copy-start(bf16[768,48]{0,1:T(8,128)(2,1)} %param.18) | copy-start | bytes 221188
  0.7 1.8 %copy-start.5 = (bf16[16,1536]{1,0:T(8,128)(2,1)S(1)}, bf16[16,1536]{1,0:T(8,128)(2,1)}, u32[]{:S(2)}) copy-start(bf16[16,1536]{1,0:T(8,128)(2,1)} %param.14) | copy-start | bytes 147460
  0.7 1.8 %copy-start.6 = (bf16[48,256]{1,0:T(8,128)(2,1)S(1)}, bf16[48,256]{1,0:T(8,128)(2,1)}, u32[]{:S(2)}) copy-start(bf16[48,256]{1,0:T(8,128)(2,1)} %wk_hbm.1) | copy-start | bytes 73732
  0.7 1.8 %copy-start.7 = (bf16[48,256]{1,0:T(8,128)(2,1)S(1)}, bf16[48,256]{1,0:T(8,128)(2,1)}, u32[]{:S(2)}) copy-start(bf16[48,256]{1,0:T(8,128)(2,1)} %wv_hbm.1) | copy-start | bytes 73732
  0.7 1.8 %copy-start.8 = (s32[16,8]{0,1:T(8,128)S(1)}, s32[16,8]{0,1:T(8,128)}, u32[]{:S(2)}) copy-start(s32[16,8]{0,1:T(8,128)} %param.24) | copy-start | bytes 1540
  0.7 1.8 %copy-start.9 = (f32[16,8]{0,1:T(8,128)S(1)}, f32[16,8]{0,1:T(8,128)}, u32[]{:S(2)}) copy-start(f32[16,8]{0,1:T(8,128)} %param.25) | copy-start | bytes 1540
  0.7 1.8 %copy-start.10 = (s32[2,64]{1,0:T(2,128)S(1)}, s32[2,64]{1,0:T(2,128)}, u32[]{:S(2)}) copy-start(s32[2,64]{1,0:T(2,128)} %par_hbm.1) | copy-start | bytes 1540
  0.7 1.8 %copy-start.11 = (s32[2]{0:T(128)S(1)}, s32[2]{0:T(128)}, u32[]{:S(2)}) copy-start(s32[2]{0:T(128)} %len_hbm.1) | copy-start | bytes 28
  0.8 1.8 %copy-start.12 = (s32[2]{0:T(128)S(1)}, s32[2]{0:T(128)}, u32[]{:S(2)}) copy-start(s32[2]{0:T(128)} %leaf_hbm.1) | copy-start | bytes 28

commit v6 on v5

--- a/solution.py
+++ b/solution.py
@@ -322,7 +322,7 @@
             part_send[:, :, r, :, i * 128 : (i + 1) * 128] = joined.astype(bf).reshape(2, 4, 8, 128)
         stat_send[:, :, r, :, :] = stat.reshape(2, 4, 8, 128)
 
-    for group, other in ((0, 1 - hi), (1, hi)):
+    def near_start(group, other):
         for d in range(1, 4):
             remote(
                 part_send.at[other, y_at[d]], near_recv.at[group, y], part_sem.at[4 * group], part_sem.at[4 * group + 1],
@@ -334,6 +334,8 @@
             ).start()
         near_recv[group, y] = part_send[other, y]
         near_stat[group, y] = stat_send[other, y]
+
+    near_start(0, 1 - hi)
 
     spread = jnp.where(
         lax.broadcasted_iota(jnp.int32, (128, HALF), 1) // 64 == lax.broadcasted_iota(jnp.int32, (128, HALF), 0), 1.0, 0.0
@@ -367,6 +369,7 @@
             row = (2 * g + parity) * 4 + x_at[d]
             remote(wout.at[row], wout.at[row], oy_out.at[0], oy_in.at[0], along_y(1 if g < 2 else 3)).start()
     near_wait(0)
+    near_start(1, hi)
     joined, stat = combine(4, near_stat[0].reshape(4, 16, 128), near_recv[0])
     far_send[...] = joined.astype(bf)
     far_stat_send[...] = stat

time: 103 us -> 104 us (level)
  Pallas kernels: 97.4 us -> 98.6 us
    pallas_call x1, Pallas kernels: 97.4 us -> 98.6 us  [local(): pl.pallas_call(layer_kernel, out_shape=(jax.ShapeDtypeStruct(tokens.shape...]
where the time goes in v6:
time: 104 us
  Pallas kernels  98.6 us (95%)
  local copies, waits for them, and re-layouts  4.29 us (4%)
    pallas_call x1, Pallas kernels, local(): pl.pallas_call(layer_kernel, out_shape=(jax.ShapeDtypeStruct(tokens.shape...  98.6 us
    unnamed x31, local copies, waits for them, and re-layouts  4.29 us

profile of v6, /device:TPU:1, one launch (start us, length us, event | category | flops | bytes accessed | tf_op | source)
XLA Modules:
  0.0 103.8 jit_solution(16977189930148416226)
XLA Ops:
  0.6 0.0 copy-start
  0.6 0.0 copy-start.1
  0.7 0.0 copy-start.2
  0.7 0.0 copy-start.3
  0.7 0.0 copy-start.4
  0.7 0.0 copy-start.5
  0.7 0.0 copy-start.6
  0.7 0.0 copy-start.7
  0.7 0.0 copy-start.8
  0.7 0.0 copy-start.9
  0.7 0.0 copy-start.10
  0.7 0.0 copy-start.11
  0.8 0.0 copy-start.12
  0.8 1.7 %copy.20 = bf16[1,1536,2,256]{3,1,2,0:T(8,128)(2,1)S(1)} copy(bf16[1,1536,2,256]{3,2,1,0:T(2,128)(2,1)} %param.26) | data formatting | bytes 3145728 | tf_op args[12]
  2.5 0.0 copy-done
  2.5 0.0 copy-done.1
  2.5 0.0 copy-done.2
  2.5 0.0 copy-done.3
  2.5 0.0 copy-done.4
  2.5 0.0 copy-done.5
  2.5 0.0 copy-done.6
  2.5 0.0 copy-done.7
  2.5 0.0 copy-done.8
  2.5 0.0 copy-done.9
  2.6 0.0 copy-done.10
  2.6 0.0 copy-done.11
  2.6 0.0 copy-done.12
  2.6 98.6 %shard_map.165 = (bf16[16,1536]{1,0:T(8,128)(2,1)S(1)}, bf16[16,1536]{1,0:T(8,128)(2,1)S(1)}, bf16[2,128,256]{2,1,0:T(8,128)(2,1)S(1)}, bf16[2,128,256]{2,1,0:T(8,128)(2,1)S(1)}) custom-call(s32[2]{0:T(128)S(1)} %copy-done.11, s32[2]{0:T(128)S(1)} %copy-done.12, bf16[2,8,1536]{2,1,0:T(8,128)(2,1)S(1)} %bitcast.13, bf16[48,768]{1,0:T(8,128)(2,1)S(1)} %copy-done.3, ...), custom_call_target="tpu_custom_call" | custom-call | tf_op jit(solution)/shard_map/pallas_call | solution.py:512
  101.2 0.6 copy.25
  101.8 0.6 copy.26
  102.5 0.7 copy.27
  103.1 0.7 copy.28
Async XLA Ops:
  0.6 1.8 %copy-start = (bf16[1,256,1536]{2,1,0:T(8,128)(2,1)S(1)}, bf16[1,256,1536]{2,1,0:T(8,128)(2,1)}, u32[]{:S(2)}) copy-start(bf16[1,256,1536]{2,1,0:T(8,128)(2,1)} %param.27) | copy-start | bytes 2359300
  0.6 1.8 %copy-start.1 = (bf16[2,128,256]{2,1,0:T(8,128)(2,1)S(1)}, bf16[2,128,256]{2,1,0:T(8,128)(2,1)}, u32[]{:S(2)}) copy-start(bf16[2,128,256]{2,1,0:T(8,128)(2,1)} %ck_hbm.1) | copy-start | bytes 393220
  0.7 1.8 %copy-start.2 = (bf16[2,128,256]{2,1,0:T(8,128)(2,1)S(1)}, bf16[2,128,256]{2,1,0:T(8,128)(2,1)}, u32[]{:S(2)}) copy-start(bf16[2,128,256]{2,1,0:T(8,128)(2,1)} %cv_hbm.1) | copy-start | bytes 393220
  0.7 1.8 %copy-start.3 = (bf16[48,768]{1,0:T(8,128)(2,1)S(1)}, bf16[48,768]{1,0:T(8,128)(2,1)}, u32[]{:S(2)}) copy-start(bf16[48,768]{1,0:T(8,128)(2,1)} %wq_hbm.1) | copy-start | bytes 221188
  0.7 1.8 %copy-start.4 = (bf16[768,48]{0,1:T(8,128)(2,1)S(1)}, bf16[768,48]{0,1:T(8,128)(2,1)}, u32[]{:S(2)}) copy-start(bf16[768,48]{0,1:T(8,128)(2,1)} %param.18) | copy-start | bytes 221188
  0.7 1.8 %copy-start.5 = (bf16[16,1536]{1,0:T(8,128)(2,1)S(1)}, bf16[16,1536]{1,0:T(8,128)(2,1)}, u32[]{:S(2)}) copy-start(bf16[16,1536]{1,0:T(8,128)(2,1)} %param.14) | copy-start | bytes 147460
  0.7 1.8 %copy-start.6 = (bf16[48,256]{1,0:T(8,128)(2,1)S(1)}, bf16[48,256]{1,0:T(8,128)(2,1)}, u32[]{:S(2)}) copy-start(bf16[48,256]{1,0:T(8,128)(2,1)} %wk_hbm.1) | copy-start | bytes 73732
  0.7 1.8 %copy-start.7 = (bf16[48,256]{1,0:T(8,128)(2,1)S(1)}, bf16[48,256]{1,0:T(8,128)(2,1)}, u32[]{:S(2)}) copy-start(bf16[48,256]{1,0:T(8,128)(2,1)} %wv_hbm.1) | copy-start | bytes 73732
  0.7 1.8 %copy-start.8 = (s32[16,8]{0,1:T(8,128)S(1)}, s32[16,8]{0,1:T(8,128)}, u32[]{:S(2)}) copy-start(s32[16,8]{0,1:T(8,128)} %param.24) | copy-start | bytes 1540
  0.7 1.8 %copy-start.9 = (f32[16,8]{0,1:T(8,128)S(1)}, f32[16,8]{0,1:T(8,128)}, u32[]{:S(2)}) copy-start(f32[16,8]{0,1:T(8,128)} %param.25) | copy-start | bytes 1540
  0.7 1.8 %copy-start.10 = (s32[2,64]{1,0:T(2,128)S(1)}, s32[2,64]{1,0:T(2,128)}, u32[]{:S(2)}) copy-start(s32[2,64]{1,0:T(2,128)} %par_hbm.1) | copy-start | bytes 1540
  0.7 1.8 %copy-start.11 = (s32[2]{0:T(128)S(1)}, s32[2]{0:T(128)}, u32[]{:S(2)}) copy-start(s32[2]{0:T(128)} %len_hbm.1) | copy-start | bytes 28
  0.8 1.8 %copy-start.12 = (s32[2]{0:T(128)S(1)}, s32[2]{0:T(128)}, u32[]{:S(2)}) copy-start(s32[2]{0:T(128)} %leaf_hbm.1) | copy-start | bytes 28
